TPU v7x, 256 devices: a whole 4x4x8 slice. The times are simulated.
256 devices in a mesh: rows: 16 (over x_lo, y, core), labels: 16 (over z, x_hi).
Axes of the slice: x: 4 (x_hi: 2, x_lo: 2; x = x_hi * 2 + x_lo), y: 4, z: 8, core: 2. Of those that a mesh axis runs over, the one named last changes fastest.
Arguments:
- points: bfloat16 [8192, 1024], P('rows'), may hold values from -6 to 6
- targets: bfloat16 [8192, 21504], P('rows', 'labels'), may hold values from -6 to 6
- coeffs: float32 [8192, 21504], P('rows', 'labels'), may hold values from -6 to 6
- block_ids: int32 [2, 512], replicated, may hold values from 0 to 8191, as said below
- inverses: float32 [2, 512, 512], replicated, as said below
Outputs:
- new_coeffs: float32 [8192, 21504], P('rows', 'labels')
Inputs may be any that keep to these rules, and one draw needn't show every extreme that they name: `block_ids`: the 512 ids of one block are distinct; the two blocks may share ids. Each inverses[b] is symmetric with a positive diagonal.
All inputs are finite; a program needn't handle non-finite values.
Results may differ from a plain program's by a relative error of at most 0.0029.
Values may be sent and summed in bfloat16 or wider, within the bound.
A program may use at most 64 MiB of HBM per device.

v0:
```python
import jax
import jax.numpy as jnp
from jax import lax
from jax.sharding import PartitionSpec as P

ridge_weight = 0.5


def kernel_tile(left, right):
    inner_prod = lax.dot_general(
        left, right, (((1,), (1,)), ((), ())), preferred_element_type=jnp.float32
    )
    left_sq = jnp.sum(jnp.square(left.astype(jnp.float32)), axis=1)
    right_sq = jnp.sum(jnp.square(right.astype(jnp.float32)), axis=1)
    sq_dist = jnp.maximum(left_sq[:, None] + right_sq[None, :] - 2.0 * inner_prod, 0.0)
    return jnp.exp(-(2.0 / left.shape[1]) * sq_dist).astype(jnp.bfloat16)


def per_device(points, targets, coeffs, block_ids, inverses):
    rows_here = points.shape[0]
    first_row = lax.axis_index("rows") * rows_here
    zero_low = jnp.zeros((), jnp.bfloat16)
    current = coeffs
    for blk in range(2):
        local_ids = block_ids[blk] - first_row
        inside = (local_ids >= 0) & (local_ids < rows_here)
        inside, local_rows = (inside, jnp.clip(local_ids, 0, rows_here - 1))
        picked = jnp.where(inside[:, None], points[local_rows], zero_low)
        block_pts = lax.psum(picked, "rows").astype(jnp.float32).astype(jnp.bfloat16)
        ktile = kernel_tile(points, block_pts)
        c_low = current.astype(jnp.bfloat16)
        sel_targets = jnp.where(inside[:, None], targets[local_rows].astype(jnp.float32), 0.0)
        sel_coeffs = jnp.where(inside[:, None], current[local_rows], 0.0)
        local_side = ridge_weight * sel_coeffs - sel_targets
        product = lax.dot_general(
            ktile, c_low, (((0,), (0,)), ((), ())), preferred_element_type=jnp.float32
        )
        negated = lax.psum(product + local_side, "rows")
        update = jnp.dot(
            inverses[blk],
            -negated,
            precision=lax.Precision.HIGHEST,
            preferred_element_type=jnp.float32,
        )
        current = current.at[local_rows].add(jnp.where(inside[:, None], update, 0.0))
    return current


def solution(mesh):
    return jax.shard_map(
        per_device,
        mesh=mesh,
        in_specs=(P("rows", None), P("rows", "labels"), P("rows", "labels"), P(), P()),
        out_specs=P("rows", "labels"),
        check_vma=False,
    )
```

profile of v0, /device:TPU:1, one launch (start us, length us, event | category | flops | bytes accessed | tf_op | source)
XLA Modules:
  0.0 487.6 jit_solution(6885395005561255958)
XLA Ops:
  6.5 0.0 all-reduce.9.cloned.1.call-start
  6.5 0.8 compare_select_fusion
  7.3 0.8 and_reduce_fusion
  8.1 0.0 copy-start
  8.1 4.2 gather_fusion
  12.3 0.0 copy-done
  12.3 2.1 gather_fusion.3
  14.4 1.6 broadcast_select_fusion
  16.0 0.0 all-reduce.9.cloned.1.call-update
  16.0 0.0 all-reduce.5.cloned.1.call-start
  16.1 2.2 copy.15
  18.3 3.0 gather_fusion.1
  21.3 2.5 copy.14
  23.8 5.6 %gather_fusion.2 = bf16[512,1344]{1,0:T(8,128)(2,1)} fusion(bf16[512,1344]{1,0:T(8,128)(2,1)} %copy.14, s32[1024]{0:T(1024)S(1)} %pad_clamp_fusion.1), kind=kCustom, calls=%fused_computation.2 | custom fusion | bytes 2754560 | tf_op jit(solution)/shard_map/gather | solution.py:32
  29.4 1.5 multiply_reduce_fusion.2
  30.9 117.6 %all-reduce.9.cloned.1.call-done = (bf16[512,1024]{1,0:T(8,128)(2,1)}, bf16[512,1024]{1,0:T(8,128)(2,1)}) async-done(((bf16[512,1024]{1,0:T(8,128)(2,1)}, bf16[512,1024]{1,0:T(8,128)(2,1)}), (bf16[512,1024]{1,0:T(8,128)(2,1)}, bf16[512,1024]{1,0:T(8,128)(2,1)})) %all-reduce.9.cloned.1.call-update) | async-done | bytes 2097168 | tf_op jit(solution)/shard_map/psum | solution.py:29
  148.6 1.5 multiply_reduce_fusion.1
  150.1 7.5 %convolution_add_fusion.1 = f32[512,1344]{1,0:T(8,128)} fusion(bf16[512,1344]{1,0:T(8,128)(2,1)} %gather_fusion.2, f32[512,1344]{1,0:T(8,128)} %gather_fusion.1, pred[512]{0:T(512)(128)(4,1)S(1)} %get-tuple-element.6, f32[512,1344]{0,1:T(8,128)} %param.7, bf16[512,1024]{1,0:T(8,128)(2,1)} %get-tuple-element.7, bf16[512,1024]{1,0:T(8,128)(2,1)} %param.5, ...), kind=kOutput, calls=%fused_computation.11 | convolution fusion | flops 1247903744 | bytes 11735552 | tf_op jit(solution)/shard_map/dot_general | solution.py:35
  157.6 0.0 all-reduce.5.cloned.1.call-update
  157.7 0.5 all-reduce.7.cloned.1.call-start
  158.2 5.6 %gather_fusion.5 = bf16[512,1344]{1,0:T(8,128)(2,1)} fusion(bf16[512,1344]{1,0:T(8,128)(2,1)} %copy.14, s32[1024]{0:T(1024)S(1)} %pad_clamp_fusion), kind=kCustom, calls=%fused_computation.5 | custom fusion | bytes 2754560 | tf_op jit(solution)/shard_map/gather | solution.py:32
  163.8 1.5 multiply_reduce_fusion
  165.3 124.0 %all-reduce.5.cloned.1.call-done = f32[512,1344]{1,0:T(8,128)} async-done(((f32[512,1344]{1,0:T(8,128)}), f32[512,1344]{1,0:T(8,128)}) %all-reduce.5.cloned.1.call-update) | async-done | bytes 2752528 | tf_op jit(solution)/shard_map/psum | solution.py:38
  289.3 12.7 %fusion = f32[512,1344]{0,1:T(8,128)} fusion(f32[512,1344]{1,0:T(8,128)} %all-reduce.5.cloned.1.call-done, pred[512]{0:T(512)(128)(4,1)S(1)} %get-tuple-element.6, f32[2,512,512]{2,1,0:T(8,128)} %param.9), kind=kOutput, calls=%fused_computation.12 | convolution fusion | flops 4229234688 | bytes 6685184 | tf_op jit(solution)/shard_map/dot_general | solution.py:39
  302.1 3.4 copy.16
  305.4 7.9 %scatter_fusion = f32[512,1344]{1,0:T(8,128)S(1)} fusion(f32[512,1344]{1,0:T(8,128)S(1)} %copy.15, s32[512]{0:T(512)S(1)} %bitcast.51, f32[512,1344]{1,0:T(8,128)} %copy.16), kind=kCustom, calls=%fused_computation.6 | custom fusion | flops 688128 | bytes 8259584 | tf_op jit(solution)/shard_map/scatter-add | solution.py:45
  313.4 3.0 gather_fusion.4
  316.4 6.5 %convolution_add_fusion = f32[512,1344]{1,0:T(8,128)} fusion(bf16[512,1344]{1,0:T(8,128)(2,1)} %gather_fusion.5, f32[512,1344]{1,0:T(8,128)} %gather_fusion.4, f32[512,1344]{1,0:T(8,128)S(1)} %scatter_fusion, pred[512]{0:T(512)(128)(4,1)S(1)} %get-tuple-element.5, bf16[512,1024]{1,0:T(8,128)(2,1)} %get-tuple-element.8, bf16[512,1024]{1,0:T(8,128)(2,1)} %param.5, ...), kind=kOutput, calls=%fused_computation.10 | convolution fusion | flops 1247903744 | bytes 11735552 | tf_op jit(solution)/shard_map/dot_general | solution.py:35
  322.8 0.0 all-reduce.7.cloned.1.call-update
  322.9 131.8 %all-reduce.7.cloned.1.call-done = f32[512,1344]{1,0:T(8,128)} async-done(((f32[512,1344]{1,0:T(8,128)}), f32[512,1344]{1,0:T(8,128)}) %all-reduce.7.cloned.1.call-update) | async-done | bytes 2752528 | tf_op jit(solution)/shard_map/psum | solution.py:38
  454.6 12.7 %fusion.1 = f32[512,1344]{0,1:T(8,128)} fusion(f32[512,1344]{1,0:T(8,128)} %all-reduce.7.cloned.1.call-done, pred[512]{0:T(512)(128)(4,1)S(1)} %get-tuple-element.5, f32[2,512,512]{2,1,0:T(8,128)} %param.9), kind=kOutput, calls=%fused_computation.13 | convolution fusion | flops 4229234688 | bytes 6685184 | tf_op jit(solution)/shard_map/dot_general | solution.py:39
  467.4 3.4 copy.18
  470.7 8.0 %scatter_fusion.1 = f32[512,1344]{1,0:T(8,128)S(1)} fusion(f32[512,1344]{1,0:T(8,128)S(1)} %scatter_fusion, s32[512]{0:T(512)S(1)} %bitcast.49, f32[512,1344]{1,0:T(8,128)} %copy.18), kind=kCustom, calls=%fused_computation.7 | custom fusion | flops 688128 | bytes 8259584 | tf_op jit(solution)/shard_map/scatter-add | solution.py:45
  478.7 2.2 copy.19
  (2 shorter events, 0.0 us)
Async XLA Ops:
  6.5 142.0 %all-reduce.9.cloned.1.call-start = ((), (), s32[]{:S(2)}) async-start(), calls=%async_computation.2 | async-start | bytes 4194304 | tf_op jit(solution)/shard_map/psum | solution.py:29
  8.1 4.2 copy-start
  16.0 273.3 %all-reduce.5.cloned.1.call-start = ((), (), s32[]{:S(2)}) async-start(), calls=%async_computation | async-start | bytes 5767168 | tf_op jit(solution)/shard_map/psum | solution.py:38
  157.7 297.0 %all-reduce.7.cloned.1.call-start = ((), (), s32[]{:S(2)}) async-start(), calls=%async_computation.1 | async-start | bytes 5767168 | tf_op jit(solution)/shard_map/psum | solution.py:38
Sparse Core Ops, SparseCore 0:
  16.1 132.3 all-reduce.8
  157.8 131.5 all-reduce.4
  323.0 131.5 all-reduce.6
where the time goes:
time: 494 us; the launch traced here: 488 us
  waiting for transfers between devices  373 us (76%)
  matrix products  39.5 us (8%)
  local copies, waits for them, and re-layouts  37.1 us (8%)
  other arithmetic  23.6 us (5%)
  between operations  13.4 us (3%)
    psum x2, waiting for transfers between devices, per_device(): negated = lax.psum(product + local_side, 'rows')  256 us
    psum x1, waiting for transfers between devices, per_device(): lax.psum(picked, 'rows').astype(jnp.float32).astype(jnp.bfloat16)  118 us
    dot_general x2, matrix products, per_device(): jnp.dot(inverses[blk], -negated, precision=lax.Precision.HIGHEST, preferr...  25.5 us
    scatter-add x2, other arithmetic, per_device(): current.at[local_rows].add(jnp.where(inside[:, None], update, 0.0))  15.9 us
    dot_general x2, matrix products, per_device(): lax.dot_general(ktile, c_low, (((0,), (0,)), ((), ())), preferred_element...  14 us
    gather x2, local copies, waits for them, and re-layouts, per_device(): targets[local_rows].astype(jnp.float32)  11.3 us
  transfers between devices with their start and end apart: 3, of which 3 were waited for; matrix products, arithmetic and copies ran while one was open for 5% of the time, Pallas kernels for 0%

commit v1 on v0

v1 whole, which is shorter than its diff:
```python
import functools

import jax
import jax.numpy as jnp
from jax import lax
from jax.experimental import pallas as pl
from jax.experimental.pallas import tpu as pltpu
from jax.sharding import PartitionSpec as P

RIDGE = 0.5
MESH = pl.DeviceIdType.MESH
F32, BF16 = jnp.float32, jnp.bfloat16
LANES = 128
WIDE = 512
COPIES = 160
NT = (((1,), (1,)), ((), ()))


def mm(a, b):
    return jnp.dot(a, b, preferred_element_type=F32)


def mm_nt(a, b):
    return lax.dot_general(a, b, NT, preferred_element_type=F32)


def split(x):
    hi = x.astype(BF16)
    return hi, (x - hi.astype(F32)).astype(BF16)


def one_hot(a, b):
    return jnp.where(a == b, 1.0, 0.0)


def row_norms(x):
    hi, lo = split(jnp.square(x.astype(F32)))
    ones = jnp.ones((8, x.shape[1]), BF16)
    return (mm_nt(ones, hi) + mm_nt(ones, lo))[0:1]


def gauss(left, right, right_norms):
    left_norms = jnp.sum(jnp.square(left.astype(F32)), axis=1, keepdims=True)
    dist = jnp.maximum(left_norms + right_norms - 2.0 * mm_nt(left, right), 0.0)
    return jnp.exp(-(2.0 / left.shape[1]) * dist).astype(BF16)


def body(cols, points, col_ids, row_ids, targets_hbm, coeffs_hbm, inverses_hbm, out_hbm, *scratch):
    n_chunks = len(cols)
    (targets, coeffs, inverses, c_low, ko, qx_send, qx_recv, qchip, qr_recv, qpiece, qbuf,
     gb_hi, gb_lo, g1_hi, g1_lo, load_sem, store_sem, send_sem, recv_sem) = scratch[:19]
    names = ("p_send", "p_own", "p_recv", "far", "rfar", "near", "rnear", "xs", "xr", "rbuf", "outv")
    bufs = [dict(zip(names, scratch[19 + len(names) * j: 19 + len(names) * (j + 1)])) for j in range(n_chunks)]

    me = lax.axis_index("rows")
    lab = lax.axis_index("labels")
    core = me % 2
    chip = me // 2
    y = chip % 4
    x = chip // 4
    z = lab // 2
    xh = lab % 2
    half = ko.shape[0] // 2
    local = points.shape[0]

    def chip_peer(d):
        return {"rows": ((chip + d) % 8) * 2 + core}

    partner = {"rows": chip * 2 + 1 - core}
    y_up = {"rows": (x * 4 + (y + 1) % 4) * 2 + core}
    y_dn = {"rows": (x * 4 + (y + 3) % 4) * 2 + core}
    x_nb = {"rows": ((1 - x) * 4 + y) * 2 + core}
    z_up = {"labels": ((z + 1) % 8) * 2 + xh}
    z_dn = {"labels": ((z + 7) % 8) * 2 + xh}

    loads = [
        pltpu.make_async_copy(coeffs_hbm, coeffs, load_sem.at[0]),
        pltpu.make_async_copy(targets_hbm, targets, load_sem.at[1]),
        pltpu.make_async_copy(inverses_hbm, inverses, load_sem.at[2]),
    ]
    for ld in loads:
        ld.start()

    barrier = pltpu.get_barrier_semaphore()
    greet = [partner, z_up, z_dn] + [chip_peer(d) for d in range(1, 8)]
    for dev in greet:
        pl.semaphore_signal(barrier, inc=1, device_id=dev, device_id_type=MESH)

    sent = []

    def push(src, dst, dev):
        i = len(sent)
        cp = pltpu.make_async_remote_copy(
            src_ref=src, dst_ref=dst, send_sem=send_sem.at[i], recv_sem=recv_sem.at[i],
            device_id=dev, device_id_type=MESH)
        cp.start()
        sent.append(cp)
        return cp

    first_row = me * local
    lane_row = first_row + lax.broadcasted_iota(jnp.int32, (1, local), 1)

    def picked(which):
        base = pl.multiple_of(z * 128 + which * 64, 64)
        sel = one_hot(col_ids[pl.ds(base, 64), :], lane_row).astype(BF16)
        return mm(sel, points[...])

    theirs = picked(1 - core).astype(BF16)
    for f in range(8):
        qx_send[f] = theirs[:, f * LANES:(f + 1) * LANES]
    pl.semaphore_wait(barrier, len(greet))
    qx = push(qx_send, qx_recv, partner)
    mine = picked(core)
    qx.wait_recv()
    for f in range(8):
        qchip[f] = (mine[:, f * LANES:(f + 1) * LANES] + qx_recv[f].astype(F32)).astype(BF16)
    red = [push(qchip.at[(chip + d) % 8], qr_recv.at[d - 1], chip_peer(d)) for d in range(1, 8)]

    point_norms = row_norms(points[...])
    loads[0].wait()
    c_low[...] = coeffs[...].astype(BF16)

    piece = qchip[chip].astype(F32)
    for d in range(1, 8):
        red[d - 1].wait_recv()
        piece = piece + qr_recv[d - 1].astype(F32)
    qpiece[...] = piece.astype(BF16)
    zrows = pl.ds(pl.multiple_of(z * 128 + core * 64, 64), 64)
    qbuf[chip, zrows, :] = piece.astype(BF16)
    gat = [push(qpiece, qbuf.at[chip, zrows, :], chip_peer(d)) for d in range(1, 8)]
    for cp in gat:
        cp.wait_recv()

    def zchunk(zz, h):
        rows = pl.ds(pl.multiple_of((zz % 8) * 128 + core * 64, 64), 64)
        ref = qbuf.at[pl.ds(4 * h, 4), rows, :]
        return ref

    shares = []

    def share_q(zz, h):
        shares.append(push(zchunk(zz, h), zchunk(zz, h), partner))

    hops = {}
    for s in range(1, 5):
        for h in range(2):
            for sign, dev in ((1, z_up), (-1, z_dn)):
                if s == 4 and (h == 0) != (sign == 1):
                    continue
                if s > 1:
                    hops[sign, s - 1, h].wait_recv()
                held = z + 8 - sign * (s - 1)
                hops[sign, s, h] = push(zchunk(held, h), zchunk(held, h), dev)
                if s == 1 and sign == 1:
                    share_q(z, h)
                elif s > 1:
                    share_q(held, h)
                if s == 4:
                    hops[sign, 3, 1 - h].wait_recv()
                    share_q(held, 1 - h)
        if s == 1:
            row = first_row + lax.broadcasted_iota(jnp.int32, (local, 1), 0)
            loads[2].wait()
            sel_t0 = one_hot(row, row_ids[:, :half]).astype(BF16)
            hi, lo = split(inverses[0])
            gb_hi[:local, :] = mm(sel_t0, hi).astype(BF16)
            gb_lo[:local, :] = mm(sel_t0, lo).astype(BF16)
        if s == 2:
            sel_t1 = one_hot(row, row_ids[:, half:]).astype(BF16)
            hi, lo = split(inverses[1])
            g1_hi[...] = mm(sel_t1, hi).astype(BF16)
            g1_lo[...] = mm(sel_t1, lo).astype(BF16)
            loads[1].wait()
    hops[1, 4, 0].wait_recv()
    share_q(z + 4, 0)
    hops[-1, 4, 1].wait_recv()
    share_q(z + 4, 1)
    for cp in shares:
        cp.wait_recv()

    def block_points(start, size):
        return jnp.concatenate([qbuf[f, pl.ds(start, size), :] for f in range(8)], axis=1)

    def left_operand(m, carry):
        start = pl.multiple_of(m * 256, 256)
        rows = pl.ds(start, 256)
        sel = one_hot(col_ids[rows, :], lane_row)
        tile = gauss(block_points(start, 256), points[...], point_norms)
        ko[rows, :local] = (tile.astype(F32) + RIDGE * sel).astype(BF16)
        ko[rows, local:] = (-sel).astype(BF16)
        return carry

    lax.fori_loop(0, 4, left_operand, 0)

    def partial(which, j):
        lo_c, w = cols[j]
        rows = pl.ds(pl.multiple_of(which * half, half), half)
        cs = slice(lo_c, lo_c + w)
        return mm(ko[rows, :local], c_low[:, cs]) + mm(ko[rows, local:], targets[:, cs])

    def yrows(step):
        return pl.ds(pl.multiple_of(((y + step) % 4) * 128, 128), 128)

    swaps = []
    for j in range(n_chunks):
        b = bufs[j]
        b["p_send"][...] = partial(1 - core, j).astype(BF16)
        swaps.append({st: push(b["p_send"].at[yrows(st), :], b["p_recv"].at[yrows(st), :], partner)
                      for st in (2, 1, 3, 0)})

    reds = [dict() for _ in range(n_chunks)]

    def chip_sum(j, st, part=None):
        b = bufs[j]
        rows = yrows(st)
        return b["p_own"][rows, :] + b["p_recv"][rows, :].astype(F32)

    for j in range(n_chunks):
        b, r = bufs[j], reds[j]
        b["p_own"][...] = partial(core, j)
        swaps[j][2].wait_recv()
        b["far"][...] = chip_sum(j, 2).astype(BF16)
        r["fu"] = push(b["far"].at[0:64, :], b["rfar"].at[0], y_up)
        r["fd"] = push(b["far"].at[64:128, :], b["rfar"].at[1], y_dn)
        swaps[j][1].wait_recv()
        up = chip_sum(j, 1)
        b["near"][1] = up[64:].astype(BF16)
        r["nu"] = push(b["near"].at[1], b["rnear"].at[0, 1], y_up)
        swaps[j][3].wait_recv()
        dn = chip_sum(j, 3)
        b["near"][2] = dn[:64].astype(BF16)
        r["nd"] = push(b["near"].at[2], b["rnear"].at[1, 0], y_dn)
        b["p_own"][yrows(1), :] = up
        b["p_own"][yrows(3), :] = dn

    q0, q1 = block_points(0, half), block_points(half, half)
    same = one_hot(col_ids[half:, :], row_ids[:, :half])
    cross = (gauss(q1, q0, row_norms(q0)).astype(F32) + RIDGE * same).astype(BF16)
    hi, lo = split(inverses[0])
    hi, lo = split(mm(cross, hi) + mm(cross, lo))
    gb_hi[local:, :] = hi
    gb_lo[local:, :] = lo

    my_rows = pl.ds(pl.multiple_of(core * half + y * 128 + x * 64, 64), 64)
    x_rows = pl.ds(pl.multiple_of(core * half + y * 128 + (1 - x) * 64, 64), 64)

    def seg(j, rows):
        return bufs[j]["rbuf"].at[rows, :]

    def seg_rows(step, xx):
        return pl.ds(pl.multiple_of(core * half + ((y + step) % 4) * 128 + xx * 64, 64), 64)

    gats = [dict() for _ in range(n_chunks)]

    def stage_dep(j):
        b, r = bufs[j], reds[j]
        r["fu"].wait_recv()
        b["near"][0] = (b["p_own"][yrows(1), :][:64] + b["rfar"][0].astype(F32)).astype(BF16)
        r["du"] = push(b["near"].at[0], b["rnear"].at[0, 0], y_up)
        r["fd"].wait_recv()
        b["near"][3] = (b["p_own"][yrows(3), :][64:] + b["rfar"][1].astype(F32)).astype(BF16)
        r["dd"] = push(b["near"].at[3], b["rnear"].at[1, 1], y_dn)

    def stage_x(j):
        b, r = bufs[j], reds[j]
        swaps[j][0].wait_recv()
        for key in ("nu", "nd", "du", "dd"):
            r[key].wait_recv()

        def total(xx):
            rows = pl.ds(pl.multiple_of(y * 128 + xx * 64, 64), 64)
            return (b["p_own"][rows, :] + b["p_recv"][rows, :].astype(F32)
                    + b["rnear"][0, xx].astype(F32) + b["rnear"][1, xx].astype(F32))

        b["xs"][...] = total(1 - x).astype(BF16)
        r["x"] = push(b["xs"], b["xr"], x_nb)
        b["p_own"][pl.ds(pl.multiple_of(y * 128, 128), 64), :] = total(x)

    def stage_r(j):
        b, r, g = bufs[j], reds[j], gats[j]
        r["x"].wait_recv()
        mine = b["p_own"][pl.ds(pl.multiple_of(y * 128, 128), 64), :]
        b["rbuf"][my_rows, :] = (mine + b["xr"][...].astype(F32)).astype(BF16)
        g["x"] = push(seg(j, my_rows), seg(j, my_rows), x_nb)
        g["u0"] = push(seg(j, my_rows), seg(j, my_rows), y_up)
        g["d0"] = push(seg(j, my_rows), seg(j, my_rows), y_dn)
        g["share"] = [push(seg(j, my_rows), seg(j, my_rows), partner)]

    def pass_on(j, rows):
        gats[j]["share"].append(push(seg(j, rows), seg(j, rows), partner))

    def stage_y(j):
        g = gats[j]
        g["x"].wait_recv()
        g["u1"] = push(seg(j, x_rows), seg(j, x_rows), y_up)
        g["d1"] = push(seg(j, x_rows), seg(j, x_rows), y_dn)
        pass_on(j, x_rows)

    def stage_fwd(j):
        g = gats[j]
        g["u0"].wait_recv()
        below = seg_rows(3, x)
        g["fu"] = push(seg(j, below), seg(j, below), y_up)
        pass_on(j, below)
        g["d1"].wait_recv()
        above = seg_rows(1, 1 - x)
        g["fd"] = push(seg(j, above), seg(j, above), y_dn)
        pass_on(j, above)
        g["d0"].wait_recv()
        pass_on(j, seg_rows(1, x))
        g["u1"].wait_recv()
        pass_on(j, seg_rows(3, 1 - x))

    def stage_last(j):
        g = gats[j]
        g["fu"].wait_recv()
        pass_on(j, seg_rows(2, x))
        g["fd"].wait_recv()
        pass_on(j, seg_rows(2, 1 - x))

    stores = []

    def stage_out(j):
        b = bufs[j]
        lo_c, w = cols[j]
        for cp in gats[j]["share"]:
            cp.wait_recv()
        n0 = b["rbuf"][:half, :]
        both = mm(gb_hi[...], n0) + mm(gb_lo[...], n0)
        w_hi, w_lo = split(b["rbuf"][half:, :].astype(F32) - both[local:])
        upd = both[:local] + mm(g1_hi[...], w_hi) + mm(g1_hi[...], w_lo) + mm(g1_lo[...], w_hi)
        b["outv"][...] = coeffs[:, lo_c:lo_c + w] - upd
        st = pltpu.make_async_copy(b["outv"], out_hbm.at[:, lo_c:lo_c + w], store_sem.at[j])
        st.start()
        stores.append(st)

    stages = [stage_dep, stage_x, stage_r, stage_y, stage_fwd, stage_last, stage_out]
    for t in range(n_chunks + len(stages) - 1):
        for k, stage in enumerate(stages):
            if 0 <= t - k < n_chunks:
                stage(t - k)

    for st in stores:
        st.wait()
    for cp in sent:
        cp.wait_send()


def per_device(points, targets, coeffs, block_ids, inverses):
    local, feat = points.shape
    labels = targets.shape[1]
    block = block_ids.shape[1]
    n = 2 * block
    ids = block_ids.reshape(n)
    cols = []
    at = 0
    while at < labels:
        w = min(WIDE, labels - at)
        cols.append((at, w))
        at += w
    vm = pltpu.VMEM
    scratch = [
        vm((local, labels), BF16), vm((local, labels), F32), vm((2, block, block), F32),
        vm((local, labels), BF16), vm((n, 2 * local), BF16),
        vm((8, 64, LANES), BF16), vm((8, 64, LANES), BF16), vm((8, 64, LANES), BF16),
        vm((7, 64, LANES), BF16), vm((64, LANES), BF16), vm((8, n, LANES), BF16),
        vm((local + block, block), BF16), vm((local + block, block), BF16),
        vm((local, block), BF16), vm((local, block), BF16),
        pltpu.SemaphoreType.DMA((3,)), pltpu.SemaphoreType.DMA((len(cols),)),
        pltpu.SemaphoreType.DMA((COPIES,)), pltpu.SemaphoreType.DMA((COPIES,)),
    ]
    for _, w in cols:
        scratch += [
            vm((block, w), BF16), vm((block, w), F32), vm((block, w), BF16),
            vm((128, w), BF16), vm((2, 64, w), BF16), vm((4, 64, w), BF16), vm((2, 2, 64, w), BF16),
            vm((64, w), BF16), vm((64, w), BF16), vm((n, w), BF16), vm((local, w), F32),
        ]
    in_vmem = pl.BlockSpec(memory_space=pltpu.VMEM)
    in_any = pl.BlockSpec(memory_space=pl.ANY)
    return pl.pallas_call(
        functools.partial(body, tuple(cols)),
        out_shape=jax.ShapeDtypeStruct((local, labels), F32),
        in_specs=[in_vmem, in_vmem, in_vmem, in_any, in_any, in_any],
        out_specs=in_any,
        scratch_shapes=scratch,
        compiler_params=pltpu.CompilerParams(
            collective_id=0, has_side_effects=True, vmem_limit_bytes=60 << 20),
        name="descent",
    )(points, ids.reshape(n, 1), ids.reshape(1, n), targets, coeffs, inverses)


def solution(mesh):
    return jax.shard_map(
        per_device,
        mesh=mesh,
        in_specs=(P("rows", None), P("rows", "labels"), P("rows", "labels"), P(), P()),
        out_specs=P("rows", "labels"),
        check_vma=False,
    )
```

time: 494 us -> 91.8 us (0.19); the launches traced: 488 us -> 91.6 us
  waiting for transfers between devices: 373 us -> 0 us
  Pallas kernels: 0 us -> 81.7 us
  matrix products: 39.5 us -> 0 us
  local copies, waits for them, and re-layouts: 37.1 us -> 9.93 us
  other arithmetic: 23.6 us -> 0 us
  between operations: 13.4 us -> 0.01 us
    psum x3 -> x0, waiting for transfers between devices: 373 us -> none  [the longest x2 256 us: per_device(): negated = lax.psum(product + local_side, 'rows')]
    pallas_call x0 -> x1, Pallas kernels: none -> 81.7 us  [per_device(): pl.pallas_call(functools.partial(body, tuple(cols)), out_shape=jax.ShapeD...]
    dot_general x4 -> x0, matrix products: 39.5 us -> none  [the longest x2 25.5 us: per_device(): jnp.dot(inverses[blk], -negated, precision=lax.Precision.HIGHEST, preferr...]
    gather x6 -> x0, local copies, waits for them, and re-layouts: 23.5 us -> none  [the longest x2 11.3 us: per_device(): targets[local_rows].astype(jnp.float32)]
    scatter-add x2 -> x0, other arithmetic: 15.9 us -> none  [per_device(): current.at[local_rows].add(jnp.where(inside[:, None], update, 0.0))]
    select_n x2 -> x0, local copies, waits for them, and re-layouts: 6.71 us -> none  [per_device(): jnp.where(inside[:, None], update, 0.0)]
  transfers between devices with their start and end apart: 3 -> 0, of which waited for: 3 -> 0; matrix products, arithmetic and copies ran while one was open for 5% -> 0% of each run, Pallas kernels for 0% -> 0%
where the time goes in v1:
time: 91.8 us; the launch traced here: 91.6 us
  Pallas kernels  81.7 us (89%)
  local copies, waits for them, and re-layouts  9.93 us (11%)
    pallas_call x1, Pallas kernels, per_device(): pl.pallas_call(functools.partial(body, tuple(cols)), out_shape=jax.ShapeD...  81.7 us
    unnamed x8, local copies, waits for them, and re-layouts  6.61 us
    pallas_call x1, local copies, waits for them, and re-layouts, per_device(): pl.pallas_call(functools.partial(body, tuple(cols)), out_shape=jax.ShapeD...  3.32 us

profile of v1, /device:TPU:1, one launch (start us, length us, event | category | flops | bytes accessed | tf_op | source)
XLA Modules:
  0.0 91.6 jit_solution(5884999938677924145)
XLA Ops:
  0.0 0.0 copy-start
  0.0 0.8 copy.13
  0.8 0.0 copy-start.1
  0.8 1.0 %copy.14 = s32[1,1024]{0,1:T(8,128)} copy(s32[1,1024]{1,0:T(1,128)S(1)} %bitcast.8) | data formatting | bytes 8192
  1.9 2.5 %copy.10.targets_hbm = bf16[512,1344]{1,0:T(8,128)(2,1)} copy(bf16[512,1344]{0,1:T(8,128)(2,1)} %param.6) | data formatting | bytes 2752512 | tf_op args[1]
  4.4 0.0 copy-done
  4.4 2.2 %copy.11.coeffs_hbm = f32[512,1344]{1,0:T(8,128)} copy(f32[512,1344]{0,1:T(8,128)S(1)} %copy-done) | data formatting | bytes 5505024 | tf_op args[2]
  6.6 0.0 copy-done.1
  6.6 81.7 %descent.1 = f32[512,1344]{1,0:T(8,128)} custom-call(bf16[512,1024]{1,0:T(8,128)(2,1)} %points.1, s32[1024,1]{1,0:T(8,128)} %bitcast.7, s32[1,1024]{1,0:T(1,128)} %bitcast.9, bf16[512,1344]{1,0:T(8,128)(2,1)} %copy.10.targets_hbm, f32[512,1344]{1,0:T(8,128)} %copy.11.coeffs_hbm, f32[2,512,512]{2,1,0:T(8,128)} %inverses_hbm.1), custom_call_target="tpu_custom_call" | custom-call | tf_op jit(solution)/shard_map/descent/pallas_call | solution.py:380
  88.3 3.3 %copy.12 = f32[512,1344]{0,1:T(8,128)} copy(f32[512,1344]{1,0:T(8,128)} %descent.1) | data formatting | bytes 5505024 | tf_op jit(solution)/shard_map/descent/pallas_call | solution.py:380
Async XLA Ops:
  0.0 4.4 %copy-start = (f32[512,1344]{0,1:T(8,128)S(1)}, f32[512,1344]{0,1:T(8,128)}, u32[]{:S(2)}) copy-start(f32[512,1344]{0,1:T(8,128)} %param.7) | copy-start | bytes 8257540
  0.8 5.8 %copy-start.1 = (s32[1,1,2,512]{3,1,2,0:T(1,128)}, s32[1,1,2,512]{3,1,2,0:T(1,128)S(1)}, u32[]{:S(2)}) copy-start(s32[1,1,2,512]{3,1,2,0:T(1,128)S(1)} %copy.13) | copy-start | bytes 12292

commit v2 on v1

v2 whole, which is shorter than its diff:
```python
import functools

import jax
import jax.numpy as jnp
from jax import lax
from jax.experimental import pallas as pl
from jax.experimental.pallas import tpu as pltpu
from jax.sharding import PartitionSpec as P

RIDGE = 0.5
MESH = pl.DeviceIdType.MESH
F32, BF16 = jnp.float32, jnp.bfloat16
LANES = 128
PARTS = ((0, 64), (64, 64), (128, 48))
SLAB = 176
COPIES = 176
NT = (((1,), (1,)), ((), ()))
TN = (((0,), (0,)), ((), ()))


def mm(a, b):
    return jnp.dot(a, b, preferred_element_type=F32)


def mm_nt(a, b):
    return lax.dot_general(a, b, NT, preferred_element_type=F32)


def split(x):
    hi = x.astype(BF16)
    return hi, (x - hi.astype(F32)).astype(BF16)


def one_hot(a, b):
    return jnp.where(a == b, 1.0, 0.0)


def row_norms(x):
    hi, lo = split(jnp.square(x.astype(F32)))
    ones = jnp.ones((8, x.shape[1]), BF16)
    return (mm_nt(ones, hi) + mm_nt(ones, lo))[0:1]


def gauss(left, right, right_norms):
    left_norms = jnp.sum(jnp.square(left.astype(F32)), axis=1, keepdims=True)
    dist = jnp.maximum(left_norms + right_norms - 2.0 * mm_nt(left, right), 0.0)
    return jnp.exp(-(2.0 / left.shape[1]) * dist).astype(BF16)


def body(points, ids, targets_hbm, coeffs_hbm, inverses_hbm, out_hbm, *scratch):
    (targets, coeffs, inverses, c_low, kt, sel, qm, qx_recv, qchip, qr_recv, qpiece, qbuf,
     weights, outv, load_sem, store_sem, send_sem, recv_sem) = scratch[:18]
    names = ("p_send", "p_own", "p_recv", "far", "rfar", "near", "rnear", "xs", "xr", "n_mine", "n_recv", "ubuf")
    bufs = [dict(zip(names, scratch[18 + len(names) * j: 18 + len(names) * (j + 1)])) for j in range(len(PARTS))]
    n_parts = len(PARTS)

    me = lax.axis_index("rows")
    lab = lax.axis_index("labels")
    core = me % 2
    chip = me // 2
    y = chip % 4
    x = chip // 4
    z = lab // 2
    xh = lab % 2
    block = ids.shape[1]
    local = points.shape[0]
    per_y = coeffs.shape[0] // 4

    def chip_peer(d):
        return {"rows": ((chip + d) % 8) * 2 + core}

    partner = {"rows": chip * 2 + 1 - core}
    y_up = {"rows": (x * 4 + (y + 1) % 4) * 2 + core}
    y_dn = {"rows": (x * 4 + (y + 3) % 4) * 2 + core}
    x_nb = {"rows": ((1 - x) * 4 + y) * 2 + core}
    z_up = {"labels": ((z + 1) % 8) * 2 + xh}
    z_dn = {"labels": ((z + 7) % 8) * 2 + xh}

    loads = [
        pltpu.make_async_copy(coeffs_hbm, coeffs, load_sem.at[0]),
        pltpu.make_async_copy(targets_hbm, targets, load_sem.at[1]),
        pltpu.make_async_copy(inverses_hbm, inverses, load_sem.at[2]),
    ]
    for ld in loads:
        ld.start()

    barrier = pltpu.get_barrier_semaphore()
    greet = [partner, z_up, z_dn] + [chip_peer(d) for d in range(1, 8)]
    for dev in greet:
        pl.semaphore_signal(barrier, inc=1, device_id=dev, device_id_type=MESH)

    sent = []

    def push(src, dst, dev):
        i = len(sent)
        cp = pltpu.make_async_remote_copy(
            src_ref=src, dst_ref=dst, send_sem=send_sem.at[i], recv_sem=recv_sem.at[i],
            device_id=dev, device_id_type=MESH)
        cp.start()
        sent.append(cp)
        return cp

    first_row = me * local
    sub_row = first_row + lax.broadcasted_iota(jnp.int32, (local, 1), 0)

    z_lanes = pl.ds(pl.multiple_of((z % 4) * 128, 128), 128)
    z_ids = jnp.where(z < 4, ids[0:1, z_lanes], ids[1:2, z_lanes])
    z_sel = one_hot(sub_row, z_ids).astype(BF16)
    found = lax.dot_general(z_sel, points[...], TN, preferred_element_type=F32).astype(BF16)
    for f in range(8):
        for h in range(2):
            qm[h, f] = found[h * 64:(h + 1) * 64, f * LANES:(f + 1) * LANES]
    pl.semaphore_wait(barrier, len(greet))
    qx = push(qm.at[1 - core], qx_recv, partner)
    for b in range(2):
        sel[b] = one_hot(sub_row, ids[b:b + 1, :]).astype(BF16)
    qx.wait_recv()
    qchip[...] = (qm[core].astype(F32) + qx_recv[...].astype(F32)).astype(BF16)
    red = [push(qchip.at[(chip + d) % 8], qr_recv.at[d - 1], chip_peer(d)) for d in range(1, 8)]

    piece = qchip[chip].astype(F32)
    for d in range(1, 8):
        red[d - 1].wait_recv()
        piece = piece + qr_recv[d - 1].astype(F32)
    qpiece[...] = piece.astype(BF16)
    zrows = pl.ds(pl.multiple_of(z * 128 + core * 64, 64), 64)
    qbuf[chip, zrows, :] = piece.astype(BF16)
    gat = [push(qpiece, qbuf.at[chip, zrows, :], chip_peer(d)) for d in range(1, 8)]
    for cp in gat:
        cp.wait_recv()

    def zchunk(zz, at, n):
        rows = pl.ds(pl.multiple_of((zz % 8) * 128 + core * 64, 64), 64)
        return qbuf.at[pl.ds(at, n), rows, :]

    shares = []

    def share_q(zz, at=0, n=8):
        shares.append(push(zchunk(zz, at, n), zchunk(zz, at, n), partner))

    hops = {}
    for s in range(1, 5):
        for h in range(4):
            for sign, dev in ((1, z_up), (-1, z_dn)):
                held = z + 8 - sign * (s - 1)
                if s > 1:
                    hops[sign, s - 1, h].wait_recv()
                if s < 4 or (h < 2) == (sign == 1):
                    hops[sign, s, h] = push(zchunk(held, 2 * h, 2), zchunk(held, 2 * h, 2), dev)
        share_q(z + 8 - (s - 1))
        if s > 1:
            share_q(z + 8 + (s - 1))
        if s == 1:
            loads[0].wait()
            c_low[...] = coeffs[...].astype(BF16)
    for sign, hs, at in ((1, (0, 1), 0), (-1, (2, 3), 4)):
        for h in hs:
            hops[sign, 4, h].wait_recv()
        share_q(z + 4, at, 4)
    for cp in shares:
        cp.wait_recv()

    def block_points(start, size):
        return jnp.concatenate([qbuf[f, pl.ds(start, size), :] for f in range(8)], axis=1)

    for b in range(2):
        q = block_points(b * block, block)
        tile = gauss(points[...], q, row_norms(q))
        kt[b] = (tile.astype(F32) + RIDGE * sel[b].astype(F32)).astype(BF16)

    loads[1].wait()

    def partial(b, st):
        rows = pl.ds(pl.multiple_of(((y + st) % 4) * per_y, 16), per_y)
        return mm(c_low[rows, :], kt[b]) - mm(targets[rows, :], sel[b])

    def put(name, st, value):
        for j, (at, h) in enumerate(PARTS):
            for xx in range(2):
                off = xx * (per_y - SLAB) + at
                ref = bufs[j][name]
                ref[pl.ds(((y + st) % 4) * 2 + xx, 1)] = value[off:off + h].astype(ref.dtype)[None]

    swaps = [dict() for _ in range(n_parts)]

    def send_half(st):
        put("p_send", st, partial(1 - core, st))
        at = pl.ds(((y + st) % 4) * 2, 2)
        for j in range(n_parts):
            swaps[j][st] = push(bufs[j]["p_send"].at[at], bufs[j]["p_recv"].at[at], partner)

    reds = [dict() for _ in range(n_parts)]

    def chip_sum(j, st, xx):
        s = ((y + st) % 4) * 2 + xx
        return bufs[j]["p_own"][s] + bufs[j]["p_recv"][s].astype(F32)

    send_half(2)
    put("p_own", 2, partial(core, 2))
    send_half(1)
    for j in range(n_parts):
        b, r = bufs[j], reds[j]
        swaps[j][2].wait_recv()
        for xx in range(2):
            b["far"][xx] = chip_sum(j, 2, xx).astype(BF16)
        r["fu"] = push(b["far"].at[0], b["rfar"].at[0], y_up)
        r["fd"] = push(b["far"].at[1], b["rfar"].at[1], y_dn)
    put("p_own", 1, partial(core, 1))
    send_half(3)
    put("p_own", 3, partial(core, 3))

    def stage_near(j):
        b, r = bufs[j], reds[j]
        swaps[j][1].wait_recv()
        b["near"][1] = chip_sum(j, 1, 1).astype(BF16)
        r["nu"] = push(b["near"].at[1], b["rnear"].at[0, 1], y_up)
        swaps[j][3].wait_recv()
        b["near"][2] = chip_sum(j, 3, 0).astype(BF16)
        r["nd"] = push(b["near"].at[2], b["rnear"].at[1, 0], y_dn)

    def stage_dep(j):
        b, r = bufs[j], reds[j]
        r["fu"].wait_recv()
        b["near"][0] = (chip_sum(j, 1, 0) + b["rfar"][0].astype(F32)).astype(BF16)
        r["du"] = push(b["near"].at[0], b["rnear"].at[0, 0], y_up)
        r["fd"].wait_recv()
        b["near"][3] = (chip_sum(j, 3, 1) + b["rfar"][1].astype(F32)).astype(BF16)
        r["dd"] = push(b["near"].at[3], b["rnear"].at[1, 1], y_dn)

    stage_near(0)
    send_half(0)
    put("p_own", 0, partial(core, 0))
    for j in range(n_parts):
        stage_dep(j)
        if j + 1 < n_parts:
            stage_near(j + 1)

    q0, q1 = block_points(0, block), block_points(block, block)
    eye = lax.broadcasted_iota(jnp.int32, (block, block), 0) == lax.broadcasted_iota(jnp.int32, (block, block), 1)
    ids0 = jnp.sum(jnp.where(eye, ids[0:1, :].astype(F32), 0.0), axis=1, keepdims=True)
    same = one_hot(ids0, ids[1:2, :].astype(F32))
    cross = (gauss(q0, q1, row_norms(q1)).astype(F32) + RIDGE * same).astype(BF16)
    loads[2].wait()
    hi, lo = split(inverses[0])
    b_hi, b_lo = split(mm(hi, cross) + mm(lo, cross))
    hi, lo = split(inverses[1])
    c_hi, c_lo = split(jnp.where(core == 1, mm(b_hi, hi) + mm(b_hi, lo) + mm(b_lo, hi), 0.0))
    weights[2] = c_hi
    weights[3] = c_lo
    hi, lo = split(inverses[core])
    weights[0] = hi
    weights[1] = lo

    def own(step, xx):
        return ((y + step) % 4) * 2 + xx

    def seg(j, s):
        return bufs[j]["ubuf"].at[core, s]

    gats = [dict() for _ in range(n_parts)]

    def stage_x(j):
        b, r = bufs[j], reds[j]
        swaps[j][0].wait_recv()
        for key in ("nu", "nd", "du", "dd"):
            r[key].wait_recv()

        def total(xx):
            return chip_sum(j, 0, xx) + b["rnear"][0, xx].astype(F32) + b["rnear"][1, xx].astype(F32)

        b["xs"][...] = total(1 - x).astype(BF16)
        r["x"] = push(b["xs"], b["xr"], x_nb)
        b["n_mine"][...] = total(x)

    def stage_swap(j):
        b, r = bufs[j], reds[j]
        r["x"].wait_recv()
        b["n_mine"][...] = b["n_mine"][...] + b["xr"][...].astype(F32)
        r["swap"] = push(b["n_mine"], b["n_recv"], partner)

    def times(n, w_hi, w_lo):
        hi, lo = split(n)
        return mm(hi, w_hi) + mm(lo, w_hi) + mm(hi, w_lo)

    def pass_on(j, s):
        gats[j]["share"].append(push(seg(j, s), seg(j, s), partner))

    def stage_u(j):
        b, r, g = bufs[j], reds[j], gats[j]
        mine = times(b["n_mine"][...], weights[0], weights[1])
        r["swap"].wait_recv()
        u = times(b["n_recv"][...], weights[2], weights[3]) - mine
        s = own(0, x)
        b["ubuf"][core, s] = u.astype(BF16)
        g["x"] = push(seg(j, s), seg(j, s), x_nb)
        g["u0"] = push(seg(j, s), seg(j, s), y_up)
        g["d0"] = push(seg(j, s), seg(j, s), y_dn)
        g["share"] = []
        pass_on(j, s)

    def stage_y(j):
        g = gats[j]
        g["x"].wait_recv()
        s = own(0, 1 - x)
        g["u1"] = push(seg(j, s), seg(j, s), y_up)
        g["d1"] = push(seg(j, s), seg(j, s), y_dn)
        pass_on(j, s)

    def stage_fwd(j):
        g = gats[j]
        g["u0"].wait_recv()
        below = own(3, x)
        g["fu"] = push(seg(j, below), seg(j, below), y_up)
        pass_on(j, below)
        g["d1"].wait_recv()
        above = own(1, 1 - x)
        g["fd"] = push(seg(j, above), seg(j, above), y_dn)
        pass_on(j, above)
        g["d0"].wait_recv()
        pass_on(j, own(1, x))
        g["u1"].wait_recv()
        pass_on(j, own(3, 1 - x))

    def stage_last(j):
        g = gats[j]
        g["fu"].wait_recv()
        pass_on(j, own(2, x))
        g["fd"].wait_recv()
        pass_on(j, own(2, 1 - x))

    stores = []

    def stage_out(j):
        ubuf = bufs[j]["ubuf"]
        at, h = PARTS[j]
        for cp in gats[j]["share"]:
            cp.wait_recv()
        upd = mm_nt(ubuf[0].reshape(8 * h, block), sel[0]) + mm_nt(ubuf[1].reshape(8 * h, block), sel[1])
        for s in range(8):
            skip = 2 * SLAB - per_y if at == 0 and s % 2 == 1 else 0
            first = (s // 2) * per_y + (s % 2) * (per_y - SLAB) + at + skip
            rows = slice(first, first + h - skip)
            outv[rows, :] = coeffs[rows, :] + upd[s * h + skip:(s + 1) * h]
            st = pltpu.make_async_copy(outv.at[rows, :], out_hbm.at[rows, :], store_sem.at[len(stores)])
            st.start()
            stores.append(st)

    stages = [stage_x, stage_swap, stage_u, stage_y, stage_fwd, stage_last, stage_out]
    for t in range(n_parts + len(stages) - 1):
        for k, stage in enumerate(stages):
            if 0 <= t - k < n_parts:
                stage(t - k)

    for st in stores:
        st.wait()
    for cp in sent:
        cp.wait_send()


def per_device(points, targets, coeffs, block_ids, inverses):
    local, feat = points.shape
    labels = targets.shape[1]
    block = block_ids.shape[1]
    n = 2 * block
    vm = pltpu.VMEM
    scratch = [
        vm((labels, local), BF16), vm((labels, local), F32), vm((2, block, block), F32),
        vm((labels, local), BF16), vm((2, local, block), BF16), vm((2, local, block), BF16),
        vm((2, 8, 64, LANES), BF16), vm((8, 64, LANES), BF16), vm((8, 64, LANES), BF16),
        vm((7, 64, LANES), BF16), vm((64, LANES), BF16), vm((8, n, LANES), BF16),
        vm((4, block, block), BF16), vm((labels, local), F32),
        pltpu.SemaphoreType.DMA((3,)), pltpu.SemaphoreType.DMA((8 * len(PARTS),)),
        pltpu.SemaphoreType.DMA((COPIES,)), pltpu.SemaphoreType.DMA((COPIES,)),
    ]
    for _, h in PARTS:
        scratch += [
            vm((8, h, block), BF16), vm((8, h, block), F32), vm((8, h, block), BF16),
            vm((2, h, block), BF16), vm((2, h, block), BF16), vm((4, h, block), BF16), vm((2, 2, h, block), BF16),
            vm((h, block), BF16), vm((h, block), BF16), vm((h, block), F32), vm((h, block), F32),
            vm((2, 8, h, block), BF16),
        ]
    in_vmem = pl.BlockSpec(memory_space=pltpu.VMEM)
    in_any = pl.BlockSpec(memory_space=pl.ANY)
    out = pl.pallas_call(
        body,
        out_shape=jax.ShapeDtypeStruct((labels, local), F32),
        in_specs=[in_vmem, in_vmem, in_any, in_any, in_any],
        out_specs=in_any,
        scratch_shapes=scratch,
        compiler_params=pltpu.CompilerParams(
            collective_id=0, has_side_effects=True, vmem_limit_bytes=60 << 20),
        name="descent",
    )(points, block_ids, targets.T, coeffs.T, inverses)
    return out.T


def solution(mesh):
    return jax.shard_map(
        per_device,
        mesh=mesh,
        in_specs=(P("rows", None), P("rows", "labels"), P("rows", "labels"), P(), P()),
        out_specs=P("rows", "labels"),
        check_vma=False,
    )
```

time: 91.8 us -> 82.9 us (0.903)
  local copies, waits for them, and re-layouts: 9.93 us -> 3.57 us
  Pallas kernels: 81.7 us -> 79.2 us
    pallas_call x1 -> x0, local copies, waits for them, and re-layouts: 3.32 us -> none  [per_device(): pl.pallas_call(functools.partial(body, tuple(cols)), out_shape=jax.ShapeD...]
    unnamed x8 -> x1, local copies, waits for them, and re-layouts: 6.61 us -> 3.57 us
    pallas_call x1, Pallas kernels: 81.7 us -> 79.2 us  [per_device(): pl.pallas_call(body, out_shape=jax.ShapeDtypeStruct((labels, local), F32)...]
where the time goes in v2:
time: 82.9 us; the launch traced here: 82.8 us
  Pallas kernels  79.2 us (96%)
  local copies, waits for them, and re-layouts  3.57 us (4%)
    pallas_call x1, Pallas kernels, per_device(): pl.pallas_call(body, out_shape=jax.ShapeDtypeStruct((labels, local), F32)...  79.2 us
    unnamed x1, local copies, waits for them, and re-layouts  3.57 us

profile of v2, /device:TPU:1, one launch (start us, length us, event | category | flops | bytes accessed | tf_op | source)
XLA Modules:
  0.0 82.8 jit_solution(12544495239501424388)
XLA Ops:
  0.0 79.2 %descent.1 = f32[1344,512]{1,0:T(8,128)} custom-call(bf16[512,1024]{1,0:T(8,128)(2,1)} %points.1, s32[2,512]{1,0:T(2,128)} %ids.1, bf16[1344,512]{1,0:T(8,128)(2,1)} %bitcast.5, f32[1344,512]{1,0:T(8,128)} %bitcast.4, f32[2,512,512]{2,1,0:T(8,128)} %inverses_hbm.1), custom_call_target="tpu_custom_call" | custom-call | tf_op jit(solution)/shard_map/descent/pallas_call | solution.py:384
  79.2 3.6 %copy.7 = f32[512,1344]{0,1:T(8,128)} copy(f32[512,1344]{0,1:T(8,128)} %bitcast.3) | data formatting | bytes 5505024

commit v3 on v2

--- a/solution.py
+++ b/solution.py
@@ -41,17 +41,20 @@
     return (mm_nt(ones, hi) + mm_nt(ones, lo))[0:1]
 
 
-def gauss(left, right, right_norms):
-    left_norms = jnp.sum(jnp.square(left.astype(F32)), axis=1, keepdims=True)
+def col_norms(x):
+    return jnp.sum(jnp.square(x.astype(F32)), axis=1, keepdims=True)
+
+
+def gauss(left, left_norms, right, right_norms):
     dist = jnp.maximum(left_norms + right_norms - 2.0 * mm_nt(left, right), 0.0)
     return jnp.exp(-(2.0 / left.shape[1]) * dist).astype(BF16)
 
 
-def body(points, ids, targets_hbm, coeffs_hbm, inverses_hbm, out_hbm, *scratch):
-    (targets, coeffs, inverses, c_low, kt, sel, qm, qx_recv, qchip, qr_recv, qpiece, qbuf,
-     weights, outv, load_sem, store_sem, send_sem, recv_sem) = scratch[:18]
+def body(points_hbm, ids_hbm, targets_hbm, coeffs_hbm, inverses_hbm, outv, *scratch):
+    (points, ids, targets, coeffs, inverses, c_low, kt, sel, qm, qx_recv, qchip, qr_recv, qpiece, qbuf,
+     weights, point_norms, load_sem, send_sem, recv_sem) = scratch[:19]
     names = ("p_send", "p_own", "p_recv", "far", "rfar", "near", "rnear", "xs", "xr", "n_mine", "n_recv", "ubuf")
-    bufs = [dict(zip(names, scratch[18 + len(names) * j: 18 + len(names) * (j + 1)])) for j in range(len(PARTS))]
+    bufs = [dict(zip(names, scratch[19 + len(names) * j: 19 + len(names) * (j + 1)])) for j in range(len(PARTS))]
     n_parts = len(PARTS)
 
     me = lax.axis_index("rows")
@@ -62,7 +65,7 @@
     x = chip // 4
     z = lab // 2
     xh = lab % 2
-    block = ids.shape[1]
+    block = ids_hbm.shape[1]
     local = points.shape[0]
     per_y = coeffs.shape[0] // 4
 
@@ -80,8 +83,10 @@
         pltpu.make_async_copy(coeffs_hbm, coeffs, load_sem.at[0]),
         pltpu.make_async_copy(targets_hbm, targets, load_sem.at[1]),
         pltpu.make_async_copy(inverses_hbm, inverses, load_sem.at[2]),
+        pltpu.make_async_copy(points_hbm, points, load_sem.at[3]),
+        pltpu.make_async_copy(ids_hbm, ids, load_sem.at[4]),
     ]
-    for ld in loads:
+    for ld in loads[::-1]:
         ld.start()
 
     barrier = pltpu.get_barrier_semaphore()
@@ -103,6 +108,8 @@
     first_row = me * local
     sub_row = first_row + lax.broadcasted_iota(jnp.int32, (local, 1), 0)
 
+    loads[4].wait()
+    loads[3].wait()
     z_lanes = pl.ds(pl.multiple_of((z % 4) * 128, 128), 128)
     z_ids = jnp.where(z < 4, ids[0:1, z_lanes], ids[1:2, z_lanes])
     z_sel = one_hot(sub_row, z_ids).astype(BF16)
@@ -137,6 +144,19 @@
 
     def share_q(zz, at=0, n=8):
         shares.append(push(zchunk(zz, at, n), zchunk(zz, at, n), partner))
+
+    def block_points(start, size):
+        return jnp.concatenate([qbuf[f, pl.ds(start, size), :] for f in range(8)], axis=1)
+
+    def fill_tile(zz, *arrived):
+        for i in arrived:
+            shares[i].wait_recv()
+        zz = zz % 8
+        lanes = pl.ds(pl.multiple_of((zz % 4) * 128, 128), 128)
+        q = block_points(pl.multiple_of(zz * 128, 128), 128)
+        tile = gauss(points[...], point_norms[...], q, row_norms(q))
+        pick = sel[zz // 4, :, lanes].astype(F32)
+        kt[zz // 4, :, lanes] = (tile.astype(F32) + RIDGE * pick).astype(BF16)
 
     hops = {}
     for s in range(1, 5):
@@ -153,20 +173,22 @@
         if s == 1:
             loads[0].wait()
             c_low[...] = coeffs[...].astype(BF16)
+            point_norms[...] = col_norms(points[...])
+        elif s == 2:
+            fill_tile(z, 0)
+        elif s == 3:
+            fill_tile(z + 7, 1)
+            fill_tile(z + 1, 2)
+        else:
+            fill_tile(z + 6, 3)
+            fill_tile(z + 2, 4)
     for sign, hs, at in ((1, (0, 1), 0), (-1, (2, 3), 4)):
         for h in hs:
             hops[sign, 4, h].wait_recv()
         share_q(z + 4, at, 4)
-    for cp in shares:
-        cp.wait_recv()
-
-    def block_points(start, size):
-        return jnp.concatenate([qbuf[f, pl.ds(start, size), :] for f in range(8)], axis=1)
-
-    for b in range(2):
-        q = block_points(b * block, block)
-        tile = gauss(points[...], q, row_norms(q))
-        kt[b] = (tile.astype(F32) + RIDGE * sel[b].astype(F32)).astype(BF16)
+    fill_tile(z + 5, 5)
+    fill_tile(z + 3, 6)
+    fill_tile(z + 4, 7, 8)
 
     loads[1].wait()
 
@@ -239,7 +261,7 @@
     eye = lax.broadcasted_iota(jnp.int32, (block, block), 0) == lax.broadcasted_iota(jnp.int32, (block, block), 1)
     ids0 = jnp.sum(jnp.where(eye, ids[0:1, :].astype(F32), 0.0), axis=1, keepdims=True)
     same = one_hot(ids0, ids[1:2, :].astype(F32))
-    cross = (gauss(q0, q1, row_norms(q1)).astype(F32) + RIDGE * same).astype(BF16)
+    cross = (gauss(q0, col_norms(q0), q1, row_norms(q1)).astype(F32) + RIDGE * same).astype(BF16)
     loads[2].wait()
     hi, lo = split(inverses[0])
     b_hi, b_lo = split(mm(hi, cross) + mm(lo, cross))
@@ -328,8 +350,6 @@
         g["fd"].wait_recv()
         pass_on(j, own(2, 1 - x))
 
-    stores = []
-
     def stage_out(j):
         ubuf = bufs[j]["ubuf"]
         at, h = PARTS[j]
@@ -341,9 +361,6 @@
             first = (s // 2) * per_y + (s % 2) * (per_y - SLAB) + at + skip
             rows = slice(first, first + h - skip)
             outv[rows, :] = coeffs[rows, :] + upd[s * h + skip:(s + 1) * h]
-            st = pltpu.make_async_copy(outv.at[rows, :], out_hbm.at[rows, :], store_sem.at[len(stores)])
-            st.start()
-            stores.append(st)
 
     stages = [stage_x, stage_swap, stage_u, stage_y, stage_fwd, stage_last, stage_out]
     for t in range(n_parts + len(stages) - 1):
@@ -351,8 +368,6 @@
             if 0 <= t - k < n_parts:
                 stage(t - k)
 
-    for st in stores:
-        st.wait()
     for cp in sent:
         cp.wait_send()
 
@@ -364,12 +379,12 @@
     n = 2 * block
     vm = pltpu.VMEM
     scratch = [
-        vm((labels, local), BF16), vm((labels, local), F32), vm((2, block, block), F32),
+        vm((local, feat), BF16), vm((2, block), jnp.int32), vm((labels, local), BF16), vm((labels, local), F32), vm((2, block, block), F32),
         vm((labels, local), BF16), vm((2, local, block), BF16), vm((2, local, block), BF16),
         vm((2, 8, 64, LANES), BF16), vm((8, 64, LANES), BF16), vm((8, 64, LANES), BF16),
         vm((7, 64, LANES), BF16), vm((64, LANES), BF16), vm((8, n, LANES), BF16),
-        vm((4, block, block), BF16), vm((labels, local), F32),
-        pltpu.SemaphoreType.DMA((3,)), pltpu.SemaphoreType.DMA((8 * len(PARTS),)),
+        vm((4, block, block), BF16), vm((local, 1), F32),
+        pltpu.SemaphoreType.DMA((5,)),
         pltpu.SemaphoreType.DMA((COPIES,)), pltpu.SemaphoreType.DMA((COPIES,)),
     ]
     for _, h in PARTS:
@@ -380,17 +395,18 @@
             vm((2, 8, h, block), BF16),
         ]
     in_vmem = pl.BlockSpec(memory_space=pltpu.VMEM)
-    in_any = pl.BlockSpec(memory_space=pl.ANY)
+    in_any = pl.BlockSpec(memory_space=pltpu.HBM)
     out = pl.pallas_call(
         body,
         out_shape=jax.ShapeDtypeStruct((labels, local), F32),
-        in_specs=[in_vmem, in_vmem, in_any, in_any, in_any],
-        out_specs=in_any,
+        in_specs=[in_any] * 5,
+        out_specs=in_vmem,
         scratch_shapes=scratch,
         compiler_params=pltpu.CompilerParams(
-            collective_id=0, has_side_effects=True, vmem_limit_bytes=60 << 20),
+            collective_id=0, has_side_effects=True, vmem_limit_bytes=44 << 20),
         name="descent",
-    )(points, block_ids, targets.T, coeffs.T, inverses)
+    )(*[pltpu.with_memory_space_constraint(a, pltpu.HBM)
+        for a in (points, block_ids, targets.T, coeffs.T, inverses)])
     return out.T
 
 

time: 82.9 us -> 77.8 us (0.938)
  Pallas kernels: 79.2 us -> 76.2 us
  local copies, waits for them, and re-layouts: 3.57 us -> 1.54 us
    pallas_call x1, Pallas kernels: 79.2 us -> 76.2 us  [per_device(): pl.pallas_call(body, out_shape=jax.ShapeDtypeStruct((labels, local), F32)...]
    unnamed x1, local copies, waits for them, and re-layouts: 3.57 us -> 1.54 us
where the time goes in v3:
time: 77.8 us; the launch traced here: 77.7 us
  Pallas kernels  76.2 us (98%)
  local copies, waits for them, and re-layouts  1.54 us (2%)
    pallas_call x1, Pallas kernels, per_device(): pl.pallas_call(body, out_shape=jax.ShapeDtypeStruct((labels, local), F32)...  76.2 us

profile of v3, /device:TPU:1, one launch (start us, length us, event | category | flops | bytes accessed | tf_op | source)
XLA Modules:
  0.0 77.7 jit_solution(17048402285639762575)
XLA Ops:
  0.0 76.2 %descent.1 = f32[1344,512]{1,0:T(8,128)S(1)} custom-call(bf16[512,1024]{1,0:T(8,128)(2,1)} %points_hbm.1, s32[2,512]{1,0:T(2,128)} %ids_hbm.1, bf16[1344,512]{1,0:T(8,128)(2,1)} %bitcast.5, f32[1344,512]{1,0:T(8,128)} %bitcast.4, f32[2,512,512]{2,1,0:T(8,128)} %inverses_hbm.1), custom_call_target="tpu_custom_call" | custom-call | tf_op jit(solution)/shard_map/descent/pallas_call | solution.py:399
  76.2 1.5 %copy.7 = f32[512,1344]{0,1:T(8,128)} copy(f32[512,1344]{0,1:T(8,128)S(1)} %bitcast.3) | data formatting | bytes 5505024

commit v4 on v3

--- a/solution.py
+++ b/solution.py
@@ -11,7 +11,7 @@
 MESH = pl.DeviceIdType.MESH
 F32, BF16 = jnp.float32, jnp.bfloat16
 LANES = 128
-PARTS = ((0, 64), (64, 64), (128, 48))
+PARTS = ((0, 64, False), (64, 64, True), (128, 48, False))
 SLAB = 176
 COPIES = 176
 NT = (((1,), (1,)), ((), ()))
@@ -53,7 +53,7 @@
 def body(points_hbm, ids_hbm, targets_hbm, coeffs_hbm, inverses_hbm, outv, *scratch):
     (points, ids, targets, coeffs, inverses, c_low, kt, sel, qm, qx_recv, qchip, qr_recv, qpiece, qbuf,
      weights, point_norms, load_sem, send_sem, recv_sem) = scratch[:19]
-    names = ("p_send", "p_own", "p_recv", "far", "rfar", "near", "rnear", "xs", "xr", "n_mine", "n_recv", "ubuf")
+    names = ("p_send", "p_own", "p_recv", "far", "rfar", "near", "rnear", "xs", "xr", "xsum", "n_mine", "n_recv", "ubuf")
     bufs = [dict(zip(names, scratch[19 + len(names) * j: 19 + len(names) * (j + 1)])) for j in range(len(PARTS))]
     n_parts = len(PARTS)
 
@@ -123,16 +123,23 @@
         sel[b] = one_hot(sub_row, ids[b:b + 1, :]).astype(BF16)
     qx.wait_recv()
     qchip[...] = (qm[core].astype(F32) + qx_recv[...].astype(F32)).astype(BF16)
-    red = [push(qchip.at[(chip + d) % 8], qr_recv.at[d - 1], chip_peer(d)) for d in range(1, 8)]
-
-    piece = qchip[chip].astype(F32)
+    par = y % 2
+
+    def group(c):
+        return (c % 2) * 4 + (c % 4 // 2) * 2 + c // 4
+
+    red = [push(qchip.at[group((chip + d) % 8)], qr_recv.at[d - 1], chip_peer(d)) for d in range(1, 8)]
+
+    mine = group(chip)
+    piece = qchip[mine].astype(F32)
     for d in range(1, 8):
         red[d - 1].wait_recv()
         piece = piece + qr_recv[d - 1].astype(F32)
     qpiece[...] = piece.astype(BF16)
     zrows = pl.ds(pl.multiple_of(z * 128 + core * 64, 64), 64)
-    qbuf[chip, zrows, :] = piece.astype(BF16)
-    gat = [push(qpiece, qbuf.at[chip, zrows, :], chip_peer(d)) for d in range(1, 8)]
+    qbuf[mine, zrows, :] = piece.astype(BF16)
+    gat = [push(qpiece, qbuf.at[mine, zrows, :], dev) for dev in
+           (x_nb, {"rows": (x * 4 + (y + 2) % 4) * 2 + core}, {"rows": ((1 - x) * 4 + (y + 2) % 4) * 2 + core})]
     for cp in gat:
         cp.wait_recv()
 
@@ -140,17 +147,10 @@
         rows = pl.ds(pl.multiple_of((zz % 8) * 128 + core * 64, 64), 64)
         return qbuf.at[pl.ds(at, n), rows, :]
 
-    shares = []
-
-    def share_q(zz, at=0, n=8):
-        shares.append(push(zchunk(zz, at, n), zchunk(zz, at, n), partner))
-
     def block_points(start, size):
         return jnp.concatenate([qbuf[f, pl.ds(start, size), :] for f in range(8)], axis=1)
 
-    def fill_tile(zz, *arrived):
-        for i in arrived:
-            shares[i].wait_recv()
+    def fill_tile(zz):
         zz = zz % 8
         lanes = pl.ds(pl.multiple_of((zz % 4) * 128, 128), 128)
         q = block_points(pl.multiple_of(zz * 128, 128), 128)
@@ -158,37 +158,70 @@
         pick = sel[zz // 4, :, lanes].astype(F32)
         kt[zz // 4, :, lanes] = (tile.astype(F32) + RIDGE * pick).astype(BF16)
 
+    shared = {}
+
+    def share_groups(k, which):
+        held = zchunk(z + 8 + k, 4 * which, 4)
+        return push(held, held, partner)
+
+    aside = {}
+
+    def y_push(k, h):
+        held = zchunk(z + 8 + k, 4 * par + 2 * h, 2)
+        aside[k, h] = push(held, held, y_up if h == 0 else y_dn)
+
+    def close(k):
+        for h in range(2):
+            aside[k, h].wait_recv()
+        shared[k] = shared[k] + [share_groups(k, 1 - par)]
+
+    def fill(k):
+        for cp in shared[k]:
+            cp.wait_recv()
+        fill_tile(z + 8 + k)
+
     hops = {}
     for s in range(1, 5):
-        for h in range(4):
+        for h in range(2):
             for sign, dev in ((1, z_up), (-1, z_dn)):
-                held = z + 8 - sign * (s - 1)
+                k = -sign * (s - 1)
                 if s > 1:
                     hops[sign, s - 1, h].wait_recv()
-                if s < 4 or (h < 2) == (sign == 1):
-                    hops[sign, s, h] = push(zchunk(held, 2 * h, 2), zchunk(held, 2 * h, 2), dev)
-        share_q(z + 8 - (s - 1))
-        if s > 1:
-            share_q(z + 8 + (s - 1))
+                if s < 4 or (h == 0) == (sign == 1):
+                    held = zchunk(z + 8 + k, 4 * par + 2 * h, 2)
+                    hops[sign, s, h] = push(held, held, dev)
+                if s > 1 or sign == 1:
+                    y_push(k, h)
+        for k in sorted({1 - s, s - 1}):
+            shared[k] = [share_groups(k, par)]
         if s == 1:
+            point_norms[...] = col_norms(points[...])
             loads[0].wait()
             c_low[...] = coeffs[...].astype(BF16)
-            point_norms[...] = col_norms(points[...])
         elif s == 2:
-            fill_tile(z, 0)
+            close(0)
         elif s == 3:
-            fill_tile(z + 7, 1)
-            fill_tile(z + 1, 2)
+            fill(0)
+            close(-1)
+            close(1)
         else:
-            fill_tile(z + 6, 3)
-            fill_tile(z + 2, 4)
-    for sign, hs, at in ((1, (0, 1), 0), (-1, (2, 3), 4)):
-        for h in hs:
-            hops[sign, 4, h].wait_recv()
-        share_q(z + 4, at, 4)
-    fill_tile(z + 5, 5)
-    fill_tile(z + 3, 6)
-    fill_tile(z + 4, 7, 8)
+            fill(-1)
+            fill(1)
+            close(-2)
+            close(2)
+    hops[1, 4, 0].wait_recv()
+    y_push(4, 0)
+    hops[-1, 4, 1].wait_recv()
+    y_push(4, 1)
+    shared[4] = [share_groups(4, par)]
+    close(-3)
+    close(3)
+    fill(-2)
+    fill(2)
+    close(4)
+    fill(-3)
+    fill(3)
+    fill(4)
 
     loads[1].wait()
 
@@ -197,7 +230,7 @@
         return mm(c_low[rows, :], kt[b]) - mm(targets[rows, :], sel[b])
 
     def put(name, st, value):
-        for j, (at, h) in enumerate(PARTS):
+        for j, (at, h, _) in enumerate(PARTS):
             for xx in range(2):
                 off = xx * (per_y - SLAB) + at
                 ref = bufs[j][name]
@@ -217,45 +250,84 @@
         s = ((y + st) % 4) * 2 + xx
         return bufs[j]["p_own"][s] + bufs[j]["p_recv"][s].astype(F32)
 
+    x_first = [mode for _, _, mode in PARTS]
+    mid = block // 2
+
+    def stage_cross(j, st):
+        b, r = bufs[j], reds[j]
+        if x_first[j]:
+            swaps[j][st].wait_recv()
+            b["xs"][st] = chip_sum(j, st, 1 - x).astype(BF16)
+            r["x", st] = push(b["xs"].at[st], b["xr"].at[st], x_nb)
+
+    def join(j, st):
+        b = bufs[j]
+        if x_first[j]:
+            reds[j]["x", st].wait_recv()
+            b["xsum"][st] = chip_sum(j, st, x) + b["xr"][st].astype(F32)
+        else:
+            swaps[j][st].wait_recv()
+
+    def val(j, st, half):
+        if x_first[j]:
+            return bufs[j]["xsum"][st, :, half * mid:(half + 1) * mid]
+        return chip_sum(j, st, half)
+
+    def stage_far(j):
+        b, r = bufs[j], reds[j]
+        join(j, 2)
+        for half in range(2):
+            b["far"][half] = val(j, 2, half).astype(BF16)
+        r["fu"] = push(b["far"].at[0], b["rfar"].at[0], y_up)
+        r["fd"] = push(b["far"].at[1], b["rfar"].at[1], y_dn)
+
+    def stage_near(j):
+        b, r = bufs[j], reds[j]
+        join(j, 1)
+        b["near"][1] = val(j, 1, 1).astype(BF16)
+        r["nu"] = push(b["near"].at[1], b["rnear"].at[0, 1], y_up)
+        join(j, 3)
+        b["near"][2] = val(j, 3, 0).astype(BF16)
+        r["nd"] = push(b["near"].at[2], b["rnear"].at[1, 0], y_dn)
+
+    def stage_dep(j):
+        b, r = bufs[j], reds[j]
+        r["fu"].wait_recv()
+        b["near"][0] = (val(j, 1, 0) + b["rfar"][0].astype(F32)).astype(BF16)
+        r["du"] = push(b["near"].at[0], b["rnear"].at[0, 0], y_up)
+        r["fd"].wait_recv()
+        b["near"][3] = (val(j, 3, 1) + b["rfar"][1].astype(F32)).astype(BF16)
+        r["dd"] = push(b["near"].at[3], b["rnear"].at[1, 1], y_dn)
+
+    y_parts = [j for j in range(n_parts) if not x_first[j]]
+    x_parts = [j for j in range(n_parts) if x_first[j]]
+
     send_half(2)
     put("p_own", 2, partial(core, 2))
     send_half(1)
-    for j in range(n_parts):
-        b, r = bufs[j], reds[j]
-        swaps[j][2].wait_recv()
-        for xx in range(2):
-            b["far"][xx] = chip_sum(j, 2, xx).astype(BF16)
-        r["fu"] = push(b["far"].at[0], b["rfar"].at[0], y_up)
-        r["fd"] = push(b["far"].at[1], b["rfar"].at[1], y_dn)
+    for j in x_parts:
+        stage_cross(j, 2)
+    for j in y_parts:
+        stage_far(j)
     put("p_own", 1, partial(core, 1))
+    for j in x_parts:
+        stage_cross(j, 1)
     send_half(3)
     put("p_own", 3, partial(core, 3))
-
-    def stage_near(j):
-        b, r = bufs[j], reds[j]
-        swaps[j][1].wait_recv()
-        b["near"][1] = chip_sum(j, 1, 1).astype(BF16)
-        r["nu"] = push(b["near"].at[1], b["rnear"].at[0, 1], y_up)
-        swaps[j][3].wait_recv()
-        b["near"][2] = chip_sum(j, 3, 0).astype(BF16)
-        r["nd"] = push(b["near"].at[2], b["rnear"].at[1, 0], y_dn)
-
-    def stage_dep(j):
-        b, r = bufs[j], reds[j]
-        r["fu"].wait_recv()
-        b["near"][0] = (chip_sum(j, 1, 0) + b["rfar"][0].astype(F32)).astype(BF16)
-        r["du"] = push(b["near"].at[0], b["rnear"].at[0, 0], y_up)
-        r["fd"].wait_recv()
-        b["near"][3] = (chip_sum(j, 3, 1) + b["rfar"][1].astype(F32)).astype(BF16)
-        r["dd"] = push(b["near"].at[3], b["rnear"].at[1, 1], y_dn)
-
-    stage_near(0)
+    stage_near(y_parts[0])
+    for j in x_parts:
+        stage_cross(j, 3)
     send_half(0)
     put("p_own", 0, partial(core, 0))
-    for j in range(n_parts):
+    stage_dep(y_parts[0])
+    for j in x_parts:
+        stage_cross(j, 0)
+        stage_far(j)
+        stage_near(j)
+    for j in y_parts[1:]:
+        stage_near(j)
+    for j in x_parts + y_parts[1:]:
         stage_dep(j)
-        if j + 1 < n_parts:
-            stage_near(j + 1)
 
     q0, q1 = block_points(0, block), block_points(block, block)
     eye = lax.broadcasted_iota(jnp.int32, (block, block), 0) == lax.broadcasted_iota(jnp.int32, (block, block), 1)
@@ -283,21 +355,26 @@
 
     def stage_x(j):
         b, r = bufs[j], reds[j]
-        swaps[j][0].wait_recv()
+        join(j, 0)
         for key in ("nu", "nd", "du", "dd"):
             r[key].wait_recv()
 
-        def total(xx):
-            return chip_sum(j, 0, xx) + b["rnear"][0, xx].astype(F32) + b["rnear"][1, xx].astype(F32)
-
-        b["xs"][...] = total(1 - x).astype(BF16)
-        r["x"] = push(b["xs"], b["xr"], x_nb)
-        b["n_mine"][...] = total(x)
+        def total(half):
+            return val(j, 0, half) + b["rnear"][0, half].astype(F32) + b["rnear"][1, half].astype(F32)
+
+        if x_first[j]:
+            b["n_mine"][:, :mid] = total(0)
+            b["n_mine"][:, mid:] = total(1)
+        else:
+            b["xs"][...] = total(1 - x).astype(BF16)
+            r["x"] = push(b["xs"], b["xr"], x_nb)
+            b["n_mine"][...] = total(x)
 
     def stage_swap(j):
         b, r = bufs[j], reds[j]
-        r["x"].wait_recv()
-        b["n_mine"][...] = b["n_mine"][...] + b["xr"][...].astype(F32)
+        if not x_first[j]:
+            r["x"].wait_recv()
+            b["n_mine"][...] = b["n_mine"][...] + b["xr"][...].astype(F32)
         r["swap"] = push(b["n_mine"], b["n_recv"], partner)
 
     def times(n, w_hi, w_lo):
@@ -320,16 +397,35 @@
         g["share"] = []
         pass_on(j, s)
 
+    def half_seg(j, s, half):
+        return bufs[j]["ubuf"].at[core, s, :, pl.ds(half * mid, mid)]
+
+    def cross(j, key, s):
+        gats[j][key] = push(seg(j, s), seg(j, s), x_nb)
+
     def stage_y(j):
         g = gats[j]
         g["x"].wait_recv()
         s = own(0, 1 - x)
-        g["u1"] = push(seg(j, s), seg(j, s), y_up)
-        g["d1"] = push(seg(j, s), seg(j, s), y_dn)
+        if not x_first[j]:
+            g["u1"] = push(seg(j, s), seg(j, s), y_up)
+            g["d1"] = push(seg(j, s), seg(j, s), y_dn)
         pass_on(j, s)
 
     def stage_fwd(j):
         g = gats[j]
+        if x_first[j]:
+            g["u0"].wait_recv()
+            below = own(3, x)
+            g["fu"] = push(half_seg(j, below, 0), half_seg(j, below, 0), y_up)
+            cross(j, "xb", below)
+            pass_on(j, below)
+            g["d0"].wait_recv()
+            above = own(1, x)
+            g["fd"] = push(half_seg(j, above, 1), half_seg(j, above, 1), y_dn)
+            cross(j, "xa", above)
+            pass_on(j, above)
+            return
         g["u0"].wait_recv()
         below = own(3, x)
         g["fu"] = push(seg(j, below), seg(j, below), y_up)
@@ -346,13 +442,27 @@
     def stage_last(j):
         g = gats[j]
         g["fu"].wait_recv()
+        if x_first[j]:
+            g["fd"].wait_recv()
+            cross(j, "xf", own(2, x))
+            pass_on(j, own(2, x))
+            g["xb"].wait_recv()
+            pass_on(j, own(3, 1 - x))
+            g["xa"].wait_recv()
+            pass_on(j, own(1, 1 - x))
+            return
         pass_on(j, own(2, x))
         g["fd"].wait_recv()
         pass_on(j, own(2, 1 - x))
 
+    def stage_end(j):
+        if x_first[j]:
+            gats[j]["xf"].wait_recv()
+            pass_on(j, own(2, 1 - x))
+
     def stage_out(j):
         ubuf = bufs[j]["ubuf"]
-        at, h = PARTS[j]
+        at, h, _ = PARTS[j]
         for cp in gats[j]["share"]:
             cp.wait_recv()
         upd = mm_nt(ubuf[0].reshape(8 * h, block), sel[0]) + mm_nt(ubuf[1].reshape(8 * h, block), sel[1])
@@ -362,7 +472,7 @@
             rows = slice(first, first + h - skip)
             outv[rows, :] = coeffs[rows, :] + upd[s * h + skip:(s + 1) * h]
 
-    stages = [stage_x, stage_swap, stage_u, stage_y, stage_fwd, stage_last, stage_out]
+    stages = [stage_x, stage_swap, stage_u, stage_y, stage_fwd, stage_last, stage_end, stage_out]
     for t in range(n_parts + len(stages) - 1):
         for k, stage in enumerate(stages):
             if 0 <= t - k < n_parts:
@@ -387,11 +497,14 @@
         pltpu.SemaphoreType.DMA((5,)),
         pltpu.SemaphoreType.DMA((COPIES,)), pltpu.SemaphoreType.DMA((COPIES,)),
     ]
-    for _, h in PARTS:
+    for _, h, x_first in PARTS:
+        w = block // 2 if x_first else block
+        crossing = (4, h, block) if x_first else (h, block)
+        kept = crossing if x_first else (8, LANES)
         scratch += [
             vm((8, h, block), BF16), vm((8, h, block), F32), vm((8, h, block), BF16),
-            vm((2, h, block), BF16), vm((2, h, block), BF16), vm((4, h, block), BF16), vm((2, 2, h, block), BF16),
-            vm((h, block), BF16), vm((h, block), BF16), vm((h, block), F32), vm((h, block), F32),
+            vm((2, h, w), BF16), vm((2, h, w), BF16), vm((4, h, w), BF16), vm((2, 2, h, w), BF16),
+            vm(crossing, BF16), vm(crossing, BF16), vm(kept, F32), vm((h, block), F32), vm((h, block), F32),
             vm((2, 8, h, block), BF16),
         ]
     in_vmem = pl.BlockSpec(memory_space=pltpu.VMEM)

time: 77.8 us -> 81.9 us (1.053)
  Pallas kernels: 76.2 us -> 80.2 us
    pallas_call x1, Pallas kernels: 76.2 us -> 80.2 us  [per_device(): pl.pallas_call(body, out_shape=jax.ShapeDtypeStruct((labels, local), F32)...]
where the time goes in v4:
time: 81.9 us; the launch traced here: 81.8 us
  Pallas kernels  80.2 us (98%)
  local copies, waits for them, and re-layouts  1.54 us (2%)
    pallas_call x1, Pallas kernels, per_device(): pl.pallas_call(body, out_shape=jax.ShapeDtypeStruct((labels, local), F32)...  80.2 us

profile of v4, /device:TPU:1, one launch (start us, length us, event | category | flops | bytes accessed | tf_op | source)
XLA Modules:
  0.0 81.8 jit_solution(13291627056683797589)
XLA Ops:
  0.0 80.2 %descent.1 = f32[1344,512]{1,0:T(8,128)S(1)} custom-call(bf16[512,1024]{1,0:T(8,128)(2,1)} %points_hbm.1, s32[2,512]{1,0:T(2,128)} %ids_hbm.1, bf16[1344,512]{1,0:T(8,128)(2,1)} %bitcast.5, f32[1344,512]{1,0:T(8,128)} %bitcast.4, f32[2,512,512]{2,1,0:T(8,128)} %inverses_hbm.1), custom_call_target="tpu_custom_call" | custom-call | tf_op jit(solution)/shard_map/descent/pallas_call | solution.py:512
  80.2 1.5 %copy.7 = f32[512,1344]{0,1:T(8,128)} copy(f32[512,1344]{0,1:T(8,128)S(1)} %bitcast.3) | data formatting | bytes 5505024

commit v5 on v3

--- a/solution.py
+++ b/solution.py
@@ -51,10 +51,10 @@
 
 
 def body(points_hbm, ids_hbm, targets_hbm, coeffs_hbm, inverses_hbm, outv, *scratch):
-    (points, ids, targets, coeffs, inverses, c_low, kt, sel, qm, qx_recv, qchip, qr_recv, qpiece, qbuf,
-     weights, point_norms, load_sem, send_sem, recv_sem) = scratch[:19]
-    names = ("p_send", "p_own", "p_recv", "far", "rfar", "near", "rnear", "xs", "xr", "n_mine", "n_recv", "ubuf")
-    bufs = [dict(zip(names, scratch[19 + len(names) * j: 19 + len(names) * (j + 1)])) for j in range(len(PARTS))]
+    (points, ids, targets, coeffs, inverses, c_low, kt, sel, pick, qm, qx_recv, qchip, qr_recv, qpiece, qbuf,
+     weights, point_norms, load_sem, send_sem, recv_sem) = scratch[:20]
+    names = ("sums", "far", "rfar", "near", "rnear", "xs", "xr", "n_mine", "n_recv", "ubuf")
+    bufs = [dict(zip(names, scratch[20 + len(names) * j: 20 + len(names) * (j + 1)])) for j in range(len(PARTS))]
     n_parts = len(PARTS)
 
     me = lax.axis_index("rows")
@@ -66,7 +66,7 @@
     z = lab // 2
     xh = lab % 2
     block = ids_hbm.shape[1]
-    local = points.shape[0]
+    local = points_hbm.shape[0]
     per_y = coeffs.shape[0] // 4
 
     def chip_peer(d):
@@ -81,9 +81,9 @@
 
     loads = [
         pltpu.make_async_copy(coeffs_hbm, coeffs, load_sem.at[0]),
-        pltpu.make_async_copy(targets_hbm, targets, load_sem.at[1]),
+        pltpu.make_async_copy(targets_hbm, targets.at[core], load_sem.at[1]),
         pltpu.make_async_copy(inverses_hbm, inverses, load_sem.at[2]),
-        pltpu.make_async_copy(points_hbm, points, load_sem.at[3]),
+        pltpu.make_async_copy(points_hbm, points.at[core], load_sem.at[3]),
         pltpu.make_async_copy(ids_hbm, ids, load_sem.at[4]),
     ]
     for ld in loads[::-1]:
@@ -110,19 +110,22 @@
 
     loads[4].wait()
     loads[3].wait()
-    z_lanes = pl.ds(pl.multiple_of((z % 4) * 128, 128), 128)
-    z_ids = jnp.where(z < 4, ids[0:1, z_lanes], ids[1:2, z_lanes])
-    z_sel = one_hot(sub_row, z_ids).astype(BF16)
-    found = lax.dot_general(z_sel, points[...], TN, preferred_element_type=F32).astype(BF16)
-    for f in range(8):
-        for h in range(2):
-            qm[h, f] = found[h * 64:(h + 1) * 64, f * LANES:(f + 1) * LANES]
+    z_lanes = pl.ds(pl.multiple_of((z // 2) * 128, 128), 128)
+    z_half = pl.ds(pl.multiple_of((z % 2) * 64, 64), 64)
+    for b in range(2):
+        z_sel = one_hot(sub_row, ids[b:b + 1, z_lanes]).astype(BF16)
+        found = lax.dot_general(z_sel, points[core], TN, preferred_element_type=F32).astype(BF16)
+        for f in range(8):
+            qm[b, f] = found[:, f * LANES:(f + 1) * LANES]
     pl.semaphore_wait(barrier, len(greet))
-    qx = push(qm.at[1 - core], qx_recv, partner)
-    for b in range(2):
-        sel[b] = one_hot(sub_row, ids[b:b + 1, :]).astype(BF16)
+    qx = push(qm.at[1 - core, :, z_half, :], qx_recv, partner)
+    lend_points = push(points.at[core], points.at[core], partner)
+    my_ids = jnp.where(core == 0, ids[0:1, :], ids[1:2, :])
+    for o in range(2):
+        chip_row = (chip * 2 + o) * local + lax.broadcasted_iota(jnp.int32, (local, 1), 0)
+        pick[o] = one_hot(chip_row, my_ids).astype(BF16)
     qx.wait_recv()
-    qchip[...] = (qm[core].astype(F32) + qx_recv[...].astype(F32)).astype(BF16)
+    qchip[...] = (qm[core, :, z_half, :].astype(F32) + qx_recv[...].astype(F32)).astype(BF16)
     red = [push(qchip.at[(chip + d) % 8], qr_recv.at[d - 1], chip_peer(d)) for d in range(1, 8)]
 
     piece = qchip[chip].astype(F32)
@@ -130,34 +133,32 @@
         red[d - 1].wait_recv()
         piece = piece + qr_recv[d - 1].astype(F32)
     qpiece[...] = piece.astype(BF16)
-    zrows = pl.ds(pl.multiple_of(z * 128 + core * 64, 64), 64)
-    qbuf[chip, zrows, :] = piece.astype(BF16)
-    gat = [push(qpiece, qbuf.at[chip, zrows, :], chip_peer(d)) for d in range(1, 8)]
+    zrows = pl.ds(pl.multiple_of(z * 64, 64), 64)
+    qbuf[core, chip, zrows, :] = piece.astype(BF16)
+    gat = [push(qpiece, qbuf.at[core, chip, zrows, :], chip_peer(d)) for d in range(1, 8)]
+    loads[1].wait()
+    lend_targets = push(targets.at[core], targets.at[core], partner)
     for cp in gat:
         cp.wait_recv()
 
     def zchunk(zz, at, n):
-        rows = pl.ds(pl.multiple_of((zz % 8) * 128 + core * 64, 64), 64)
-        return qbuf.at[pl.ds(at, n), rows, :]
-
-    shares = []
-
-    def share_q(zz, at=0, n=8):
-        shares.append(push(zchunk(zz, at, n), zchunk(zz, at, n), partner))
-
-    def block_points(start, size):
-        return jnp.concatenate([qbuf[f, pl.ds(start, size), :] for f in range(8)], axis=1)
-
-    def fill_tile(zz, *arrived):
-        for i in arrived:
-            shares[i].wait_recv()
-        zz = zz % 8
-        lanes = pl.ds(pl.multiple_of((zz % 4) * 128, 128), 128)
-        q = block_points(pl.multiple_of(zz * 128, 128), 128)
-        tile = gauss(points[...], point_norms[...], q, row_norms(q))
-        pick = sel[zz // 4, :, lanes].astype(F32)
-        kt[zz // 4, :, lanes] = (tile.astype(F32) + RIDGE * pick).astype(BF16)
-
+        rows = pl.ds(pl.multiple_of((zz % 8) * 64, 64), 64)
+        return qbuf.at[core, pl.ds(at, n), rows, :]
+
+    def block_points(b, start, size):
+        return jnp.concatenate([qbuf[b, f, pl.ds(start, size), :] for f in range(8)], axis=1)
+
+    def fill_tile(pair):
+        at = pl.multiple_of((pair % 4) * 128, 128)
+        q = block_points(core, at, 128)
+        norms = row_norms(q)
+        lanes = pl.ds(at, 128)
+        for o in range(2):
+            tile = gauss(points[o], point_norms[o], q, norms)
+            kt[o, :, lanes] = (tile.astype(F32) + RIDGE * pick[o, :, lanes].astype(F32)).astype(BF16)
+
+    pair = z // 2 + 4
+    lean = 2 * (z % 2) - 1
     hops = {}
     for s in range(1, 5):
         for h in range(4):
@@ -167,76 +168,57 @@
                     hops[sign, s - 1, h].wait_recv()
                 if s < 4 or (h < 2) == (sign == 1):
                     hops[sign, s, h] = push(zchunk(held, 2 * h, 2), zchunk(held, 2 * h, 2), dev)
-        share_q(z + 8 - (s - 1))
-        if s > 1:
-            share_q(z + 8 + (s - 1))
         if s == 1:
             loads[0].wait()
-            c_low[...] = coeffs[...].astype(BF16)
-            point_norms[...] = col_norms(points[...])
+            c_low[core] = coeffs[...].astype(BF16)
+            lend_low = push(c_low.at[core], c_low.at[core], partner)
+            lend_points.wait_recv()
+            for o in range(2):
+                point_norms[o] = col_norms(points[o])
         elif s == 2:
-            fill_tile(z, 0)
+            fill_tile(pair)
+            for b in range(2):
+                sel[b] = one_hot(sub_row, ids[b:b + 1, :]).astype(BF16)
         elif s == 3:
-            fill_tile(z + 7, 1)
-            fill_tile(z + 1, 2)
+            fill_tile(pair + lean)
         else:
-            fill_tile(z + 6, 3)
-            fill_tile(z + 2, 4)
-    for sign, hs, at in ((1, (0, 1), 0), (-1, (2, 3), 4)):
+            fill_tile(pair - lean)
+    for sign, hs in ((1, (0, 1)), (-1, (2, 3))):
         for h in hs:
             hops[sign, 4, h].wait_recv()
-        share_q(z + 4, at, 4)
-    fill_tile(z + 5, 5)
-    fill_tile(z + 3, 6)
-    fill_tile(z + 4, 7, 8)
-
-    loads[1].wait()
-
-    def partial(b, st):
+    lend_block = push(qbuf.at[core], qbuf.at[core], partner)
+    fill_tile(pair + 2)
+    lend_targets.wait_recv()
+    lend_low.wait_recv()
+
+    def partial(st):
         rows = pl.ds(pl.multiple_of(((y + st) % 4) * per_y, 16), per_y)
-        return mm(c_low[rows, :], kt[b]) - mm(targets[rows, :], sel[b])
-
-    def put(name, st, value):
+        value = (mm(c_low[0, rows, :], kt[0]) + mm(c_low[1, rows, :], kt[1])
+                 - mm(targets[0, rows, :], pick[0]) - mm(targets[1, rows, :], pick[1]))
         for j, (at, h) in enumerate(PARTS):
             for xx in range(2):
                 off = xx * (per_y - SLAB) + at
-                ref = bufs[j][name]
-                ref[pl.ds(((y + st) % 4) * 2 + xx, 1)] = value[off:off + h].astype(ref.dtype)[None]
-
-    swaps = [dict() for _ in range(n_parts)]
-
-    def send_half(st):
-        put("p_send", st, partial(1 - core, st))
-        at = pl.ds(((y + st) % 4) * 2, 2)
-        for j in range(n_parts):
-            swaps[j][st] = push(bufs[j]["p_send"].at[at], bufs[j]["p_recv"].at[at], partner)
+                bufs[j]["sums"][pl.ds(((y + st) % 4) * 2 + xx, 1)] = value[off:off + h][None]
 
     reds = [dict() for _ in range(n_parts)]
 
     def chip_sum(j, st, xx):
-        s = ((y + st) % 4) * 2 + xx
-        return bufs[j]["p_own"][s] + bufs[j]["p_recv"][s].astype(F32)
-
-    send_half(2)
-    put("p_own", 2, partial(core, 2))
-    send_half(1)
+        return bufs[j]["sums"][((y + st) % 4) * 2 + xx]
+
+    partial(2)
     for j in range(n_parts):
         b, r = bufs[j], reds[j]
-        swaps[j][2].wait_recv()
         for xx in range(2):
             b["far"][xx] = chip_sum(j, 2, xx).astype(BF16)
         r["fu"] = push(b["far"].at[0], b["rfar"].at[0], y_up)
         r["fd"] = push(b["far"].at[1], b["rfar"].at[1], y_dn)
-    put("p_own", 1, partial(core, 1))
-    send_half(3)
-    put("p_own", 3, partial(core, 3))
+    partial(1)
+    partial(3)
 
     def stage_near(j):
         b, r = bufs[j], reds[j]
-        swaps[j][1].wait_recv()
         b["near"][1] = chip_sum(j, 1, 1).astype(BF16)
         r["nu"] = push(b["near"].at[1], b["rnear"].at[0, 1], y_up)
-        swaps[j][3].wait_recv()
         b["near"][2] = chip_sum(j, 3, 0).astype(BF16)
         r["nd"] = push(b["near"].at[2], b["rnear"].at[1, 0], y_dn)
 
@@ -250,14 +232,14 @@
         r["dd"] = push(b["near"].at[3], b["rnear"].at[1, 1], y_dn)
 
     stage_near(0)
-    send_half(0)
-    put("p_own", 0, partial(core, 0))
+    partial(0)
     for j in range(n_parts):
         stage_dep(j)
         if j + 1 < n_parts:
             stage_near(j + 1)
 
-    q0, q1 = block_points(0, block), block_points(block, block)
+    lend_block.wait_recv()
+    q0, q1 = block_points(0, 0, block), block_points(1, 0, block)
     eye = lax.broadcasted_iota(jnp.int32, (block, block), 0) == lax.broadcasted_iota(jnp.int32, (block, block), 1)
     ids0 = jnp.sum(jnp.where(eye, ids[0:1, :].astype(F32), 0.0), axis=1, keepdims=True)
     same = one_hot(ids0, ids[1:2, :].astype(F32))
@@ -283,7 +265,6 @@
 
     def stage_x(j):
         b, r = bufs[j], reds[j]
-        swaps[j][0].wait_recv()
         for key in ("nu", "nd", "du", "dd"):
             r[key].wait_recv()
 
@@ -379,17 +360,17 @@
     n = 2 * block
     vm = pltpu.VMEM
     scratch = [
-        vm((local, feat), BF16), vm((2, block), jnp.int32), vm((labels, local), BF16), vm((labels, local), F32), vm((2, block, block), F32),
-        vm((labels, local), BF16), vm((2, local, block), BF16), vm((2, local, block), BF16),
-        vm((2, 8, 64, LANES), BF16), vm((8, 64, LANES), BF16), vm((8, 64, LANES), BF16),
-        vm((7, 64, LANES), BF16), vm((64, LANES), BF16), vm((8, n, LANES), BF16),
-        vm((4, block, block), BF16), vm((local, 1), F32),
+        vm((2, local, feat), BF16), vm((2, block), jnp.int32), vm((2, labels, local), BF16), vm((labels, local), F32),
+        vm((2, block, block), F32), vm((2, labels, local), BF16), vm((2, local, block), BF16), vm((2, local, block), BF16),
+        vm((2, local, block), BF16), vm((2, 8, 128, LANES), BF16), vm((8, 64, LANES), BF16), vm((8, 64, LANES), BF16),
+        vm((7, 64, LANES), BF16), vm((64, LANES), BF16), vm((2, 8, block, LANES), BF16),
+        vm((4, block, block), BF16), vm((2, local, 1), F32),
         pltpu.SemaphoreType.DMA((5,)),
         pltpu.SemaphoreType.DMA((COPIES,)), pltpu.SemaphoreType.DMA((COPIES,)),
     ]
     for _, h in PARTS:
         scratch += [
-            vm((8, h, block), BF16), vm((8, h, block), F32), vm((8, h, block), BF16),
+            vm((8, h, block), F32),
             vm((2, h, block), BF16), vm((2, h, block), BF16), vm((4, h, block), BF16), vm((2, 2, h, block), BF16),
             vm((h, block), BF16), vm((h, block), BF16), vm((h, block), F32), vm((h, block), F32),
             vm((2, 8, h, block), BF16),

time: 77.8 us -> 73.2 us (0.941)
  Pallas kernels: 76.2 us -> 71.5 us
    pallas_call x1, Pallas kernels: 76.2 us -> 71.5 us  [per_device(): pl.pallas_call(body, out_shape=jax.ShapeDtypeStruct((labels, local), F32)...]
where the time goes in v5:
time: 73.2 us; the launch traced here: 73.1 us
  Pallas kernels  71.5 us (98%)
  local copies, waits for them, and re-layouts  1.54 us (2%)
    pallas_call x1, Pallas kernels, per_device(): pl.pallas_call(body, out_shape=jax.ShapeDtypeStruct((labels, local), F32)...  71.5 us
    unnamed x1, local copies, waits for them, and re-layouts  1.54 us

profile of v5, /device:TPU:1, one launch (start us, length us, event | category | flops | bytes accessed | tf_op | source)
XLA Modules:
  0.0 73.1 jit_solution(15312499184261617219)
XLA Ops:
  0.0 71.5 %descent.1 = f32[1344,512]{1,0:T(8,128)S(1)} custom-call(bf16[512,1024]{1,0:T(8,128)(2,1)} %points_hbm.1, s32[2,512]{1,0:T(2,128)} %ids_hbm.1, bf16[1344,512]{1,0:T(8,128)(2,1)} %bitcast.5, f32[1344,512]{1,0:T(8,128)} %bitcast.4, f32[2,512,512]{2,1,0:T(8,128)} %inverses_hbm.1), custom_call_target="tpu_custom_call" | custom-call | tf_op jit(solution)/shard_map/descent/pallas_call | solution.py:380
  71.5 1.5 %copy.7 = f32[512,1344]{0,1:T(8,128)} copy(f32[512,1344]{0,1:T(8,128)S(1)} %bitcast.3) | data formatting | bytes 5505024

commit v6 on v5

--- a/solution.py
+++ b/solution.py
@@ -51,10 +51,11 @@
 
 
 def body(points_hbm, ids_hbm, targets_hbm, coeffs_hbm, inverses_hbm, outv, *scratch):
-    (points, ids, targets, coeffs, inverses, c_low, kt, sel, pick, qm, qx_recv, qchip, qr_recv, qpiece, qbuf,
-     weights, point_norms, load_sem, send_sem, recv_sem) = scratch[:20]
-    names = ("sums", "far", "rfar", "near", "rnear", "xs", "xr", "n_mine", "n_recv", "ubuf")
-    bufs = [dict(zip(names, scratch[20 + len(names) * j: 20 + len(names) * (j + 1)])) for j in range(len(PARTS))]
+    (points, ids, targets, coeffs, inverses, c_low, sel, qm, qx_recv, qchip, qr_recv, qpiece, qbuf,
+     weights, point_norms, load_sem, near_sem, send_sem, recv_sem) = scratch[:19]
+    names = ("kt", "pick", "sums", "far", "rfar", "near", "rnear", "xs", "xr", "n_mine", "n_recv")
+    bufs = [dict(zip(names, scratch[19 + len(names) * p: 19 + len(names) * (p + 1)])) for p in range(2)]
+    ubufs = scratch[19 + 2 * len(names):]
     n_parts = len(PARTS)
 
     me = lax.axis_index("rows")
@@ -75,6 +76,9 @@
     partner = {"rows": chip * 2 + 1 - core}
     y_up = {"rows": (x * 4 + (y + 1) % 4) * 2 + core}
     y_dn = {"rows": (x * 4 + (y + 3) % 4) * 2 + core}
+    def at_chip(xx, step):
+        return {"rows": (xx * 4 + (y + step) % 4) * 2 + core}
+
     x_nb = {"rows": ((1 - x) * 4 + y) * 2 + core}
     z_up = {"labels": ((z + 1) % 8) * 2 + xh}
     z_dn = {"labels": ((z + 7) % 8) * 2 + xh}
@@ -96,10 +100,10 @@
 
     sent = []
 
-    def push(src, dst, dev):
+    def push(src, dst, dev, slot=None):
         i = len(sent)
         cp = pltpu.make_async_remote_copy(
-            src_ref=src, dst_ref=dst, send_sem=send_sem.at[i], recv_sem=recv_sem.at[i],
+            src_ref=src, dst_ref=dst, send_sem=send_sem.at[i], recv_sem=recv_sem.at[i] if slot is None else near_sem.at[slot],
             device_id=dev, device_id_type=MESH)
         cp.start()
         sent.append(cp)
@@ -120,10 +124,6 @@
     pl.semaphore_wait(barrier, len(greet))
     qx = push(qm.at[1 - core, :, z_half, :], qx_recv, partner)
     lend_points = push(points.at[core], points.at[core], partner)
-    my_ids = jnp.where(core == 0, ids[0:1, :], ids[1:2, :])
-    for o in range(2):
-        chip_row = (chip * 2 + o) * local + lax.broadcasted_iota(jnp.int32, (local, 1), 0)
-        pick[o] = one_hot(chip_row, my_ids).astype(BF16)
     qx.wait_recv()
     qchip[...] = (qm[core, :, z_half, :].astype(F32) + qx_recv[...].astype(F32)).astype(BF16)
     red = [push(qchip.at[(chip + d) % 8], qr_recv.at[d - 1], chip_peer(d)) for d in range(1, 8)]
@@ -148,14 +148,75 @@
     def block_points(b, start, size):
         return jnp.concatenate([qbuf[b, f, pl.ds(start, size), :] for f in range(8)], axis=1)
 
-    def fill_tile(pair):
+    def fill_tile(p, i, pair):
         at = pl.multiple_of((pair % 4) * 128, 128)
         q = block_points(core, at, 128)
         norms = row_norms(q)
-        lanes = pl.ds(at, 128)
+        pair_ids = jnp.where(core == 0, ids[0:1, pl.ds(at, 128)], ids[1:2, pl.ds(at, 128)])
         for o in range(2):
+            chip_row = (chip * 2 + o) * local + lax.broadcasted_iota(jnp.int32, (local, 1), 0)
+            hit = one_hot(chip_row, pair_ids)
             tile = gauss(points[o], point_norms[o], q, norms)
-            kt[o, :, lanes] = (tile.astype(F32) + RIDGE * pick[o, :, lanes].astype(F32)).astype(BF16)
+            bufs[p]["kt"][o, :, i * 128:(i + 1) * 128] = (tile.astype(F32) + RIDGE * hit).astype(BF16)
+            bufs[p]["pick"][o, :, i * 128:(i + 1) * 128] = hit.astype(BF16)
+
+    reds = [dict() for _ in range(2)]
+
+    def partial(p, st):
+        b = bufs[p]
+        rows = pl.ds(pl.multiple_of(((y + st) % 4) * per_y, 16), per_y)
+        value = (mm(c_low[0, rows, :], b["kt"][0]) + mm(c_low[1, rows, :], b["kt"][1])
+                 - mm(targets[0, rows, :], b["pick"][0]) - mm(targets[1, rows, :], b["pick"][1]))
+        for xx in range(2):
+            off = xx * (per_y - SLAB)
+            b["sums"][pl.ds(((y + st) % 4) * 2 + xx, 1)] = value[off:off + SLAB][None]
+
+    def chip_sum(p, st, xx):
+        return bufs[p]["sums"][((y + st) % 4) * 2 + xx]
+
+    def near(p, k, way, value, xx):
+        b = bufs[p]
+        b["near"][k] = value.astype(BF16)
+        push(b["near"].at[k], b["rnear"].at[way, x], at_chip(xx, 1 if way == 0 else 3), 4 * p + 2 * way + x)
+
+    def stage_far(p):
+        b, r = bufs[p], reds[p]
+        partial(p, 2)
+        for xx in range(2):
+            b["far"][xx] = chip_sum(p, 2, xx).astype(BF16)
+        r["fu"] = push(b["far"].at[0], b["rfar"].at[0], y_up)
+        r["fd"] = push(b["far"].at[1], b["rfar"].at[1], y_dn)
+
+    def stage_near(p):
+        b, r = bufs[p], reds[p]
+        partial(p, 1)
+        near(p, 1, 0, chip_sum(p, 1, 1), 1)
+        partial(p, 3)
+        near(p, 2, 1, chip_sum(p, 3, 0), 0)
+        partial(p, 0)
+        b["xs"][...] = chip_sum(p, 0, 1 - x).astype(BF16)
+        r["x"] = push(b["xs"], b["xr"], x_nb)
+
+    def stage_dep(p):
+        b, r = bufs[p], reds[p]
+        r["fu"].wait_recv()
+        near(p, 0, 0, chip_sum(p, 1, 0) + b["rfar"][0].astype(F32), 0)
+        r["fd"].wait_recv()
+        near(p, 3, 1, chip_sum(p, 3, 1) + b["rfar"][1].astype(F32), 1)
+
+    def stage_swap(p):
+        b, r = bufs[p], reds[p]
+        total = chip_sum(p, 0, x)
+        r["x"].wait_recv()
+        total = total + b["xr"][...].astype(F32)
+        for way in range(2):
+            for src in range(2):
+                pltpu.make_async_remote_copy(
+                    src_ref=b["near"].at[0], dst_ref=b["rnear"].at[way, src], send_sem=send_sem.at[0],
+                    recv_sem=near_sem.at[4 * p + 2 * way + src], device_id=x_nb, device_id_type=MESH).wait_recv()
+                total = total + b["rnear"][way, src].astype(F32)
+        b["n_mine"][...] = total
+        r["swap"] = push(b["n_mine"], b["n_recv"], partner)
 
     pair = z // 2 + 4
     lean = 2 * (z % 2) - 1
@@ -176,82 +237,48 @@
             for o in range(2):
                 point_norms[o] = col_norms(points[o])
         elif s == 2:
-            fill_tile(pair)
+            fill_tile(0, 0, pair)
             for b in range(2):
                 sel[b] = one_hot(sub_row, ids[b:b + 1, :]).astype(BF16)
         elif s == 3:
-            fill_tile(pair + lean)
+            fill_tile(0, 1, pair + lean)
+            lend_targets.wait_recv()
+            lend_low.wait_recv()
+            stage_far(0)
+            stage_near(0)
         else:
-            fill_tile(pair - lean)
+            fill_tile(1, 0, pair - lean)
+            stage_dep(0)
     for sign, hs in ((1, (0, 1)), (-1, (2, 3))):
         for h in hs:
             hops[sign, 4, h].wait_recv()
     lend_block = push(qbuf.at[core], qbuf.at[core], partner)
-    fill_tile(pair + 2)
-    lend_targets.wait_recv()
-    lend_low.wait_recv()
-
-    def partial(st):
-        rows = pl.ds(pl.multiple_of(((y + st) % 4) * per_y, 16), per_y)
-        value = (mm(c_low[0, rows, :], kt[0]) + mm(c_low[1, rows, :], kt[1])
-                 - mm(targets[0, rows, :], pick[0]) - mm(targets[1, rows, :], pick[1]))
-        for j, (at, h) in enumerate(PARTS):
-            for xx in range(2):
-                off = xx * (per_y - SLAB) + at
-                bufs[j]["sums"][pl.ds(((y + st) % 4) * 2 + xx, 1)] = value[off:off + h][None]
-
-    reds = [dict() for _ in range(n_parts)]
-
-    def chip_sum(j, st, xx):
-        return bufs[j]["sums"][((y + st) % 4) * 2 + xx]
-
-    partial(2)
-    for j in range(n_parts):
-        b, r = bufs[j], reds[j]
-        for xx in range(2):
-            b["far"][xx] = chip_sum(j, 2, xx).astype(BF16)
-        r["fu"] = push(b["far"].at[0], b["rfar"].at[0], y_up)
-        r["fd"] = push(b["far"].at[1], b["rfar"].at[1], y_dn)
-    partial(1)
-    partial(3)
-
-    def stage_near(j):
-        b, r = bufs[j], reds[j]
-        b["near"][1] = chip_sum(j, 1, 1).astype(BF16)
-        r["nu"] = push(b["near"].at[1], b["rnear"].at[0, 1], y_up)
-        b["near"][2] = chip_sum(j, 3, 0).astype(BF16)
-        r["nd"] = push(b["near"].at[2], b["rnear"].at[1, 0], y_dn)
-
-    def stage_dep(j):
-        b, r = bufs[j], reds[j]
-        r["fu"].wait_recv()
-        b["near"][0] = (chip_sum(j, 1, 0) + b["rfar"][0].astype(F32)).astype(BF16)
-        r["du"] = push(b["near"].at[0], b["rnear"].at[0, 0], y_up)
-        r["fd"].wait_recv()
-        b["near"][3] = (chip_sum(j, 3, 1) + b["rfar"][1].astype(F32)).astype(BF16)
-        r["dd"] = push(b["near"].at[3], b["rnear"].at[1, 1], y_dn)
-
-    stage_near(0)
-    partial(0)
-    for j in range(n_parts):
-        stage_dep(j)
-        if j + 1 < n_parts:
-            stage_near(j + 1)
-
+    fill_tile(1, 1, pair + 2)
+    stage_far(1)
+    stage_near(1)
+    stage_swap(0)
+    stage_dep(1)
     lend_block.wait_recv()
+
     q0, q1 = block_points(0, 0, block), block_points(1, 0, block)
     eye = lax.broadcasted_iota(jnp.int32, (block, block), 0) == lax.broadcasted_iota(jnp.int32, (block, block), 1)
     ids0 = jnp.sum(jnp.where(eye, ids[0:1, :].astype(F32), 0.0), axis=1, keepdims=True)
     same = one_hot(ids0, ids[1:2, :].astype(F32))
     cross = (gauss(q0, col_norms(q0), q1, row_norms(q1)).astype(F32) + RIDGE * same).astype(BF16)
     loads[2].wait()
-    hi, lo = split(inverses[0])
+
+    def arrival_rows(b):
+        order = (pair, pair + lean, pair - lean, pair + 2)
+        return jnp.concatenate(
+            [inverses[b, pl.ds(pl.multiple_of((g % 4) * 128, 128), 128), :] for g in order], axis=0)
+
+    hi, lo = split(arrival_rows(0))
     b_hi, b_lo = split(mm(hi, cross) + mm(lo, cross))
     hi, lo = split(inverses[1])
     c_hi, c_lo = split(jnp.where(core == 1, mm(b_hi, hi) + mm(b_hi, lo) + mm(b_lo, hi), 0.0))
     weights[2] = c_hi
     weights[3] = c_lo
-    hi, lo = split(inverses[core])
+    hi, lo = split(arrival_rows(core))
     weights[0] = hi
     weights[1] = lo
 
@@ -259,27 +286,9 @@
         return ((y + step) % 4) * 2 + xx
 
     def seg(j, s):
-        return bufs[j]["ubuf"].at[core, s]
+        return ubufs[j].at[core, s]
 
     gats = [dict() for _ in range(n_parts)]
-
-    def stage_x(j):
-        b, r = bufs[j], reds[j]
-        for key in ("nu", "nd", "du", "dd"):
-            r[key].wait_recv()
-
-        def total(xx):
-            return chip_sum(j, 0, xx) + b["rnear"][0, xx].astype(F32) + b["rnear"][1, xx].astype(F32)
-
-        b["xs"][...] = total(1 - x).astype(BF16)
-        r["x"] = push(b["xs"], b["xr"], x_nb)
-        b["n_mine"][...] = total(x)
-
-    def stage_swap(j):
-        b, r = bufs[j], reds[j]
-        r["x"].wait_recv()
-        b["n_mine"][...] = b["n_mine"][...] + b["xr"][...].astype(F32)
-        r["swap"] = push(b["n_mine"], b["n_recv"], partner)
 
     def times(n, w_hi, w_lo):
         hi, lo = split(n)
@@ -288,16 +297,26 @@
     def pass_on(j, s):
         gats[j]["share"].append(push(seg(j, s), seg(j, s), partner))
 
+    stage_swap(1)
+
+    def rows_of(j, name):
+        at, h = PARTS[j]
+        return jnp.concatenate([bufs[p][name][at:at + h, :] for p in range(2)], axis=1)
+
     def stage_u(j):
-        b, r, g = bufs[j], reds[j], gats[j]
-        mine = times(b["n_mine"][...], weights[0], weights[1])
-        r["swap"].wait_recv()
-        u = times(b["n_recv"][...], weights[2], weights[3]) - mine
+        g = gats[j]
+        mine = times(rows_of(j, "n_mine"), weights[0], weights[1])
+        if j == 0:
+            for p in range(2):
+                reds[p]["swap"].wait_recv()
+        u = times(rows_of(j, "n_recv"), weights[2], weights[3]) - mine
         s = own(0, x)
-        b["ubuf"][core, s] = u.astype(BF16)
+        ubufs[j][core, s] = u.astype(BF16)
         g["x"] = push(seg(j, s), seg(j, s), x_nb)
         g["u0"] = push(seg(j, s), seg(j, s), y_up)
         g["d0"] = push(seg(j, s), seg(j, s), y_dn)
+        g["u1"] = push(seg(j, s), seg(j, s), at_chip(1 - x, 1))
+        g["d1"] = push(seg(j, s), seg(j, s), at_chip(1 - x, 3))
         g["share"] = []
         pass_on(j, s)
 
@@ -305,8 +324,6 @@
         g = gats[j]
         g["x"].wait_recv()
         s = own(0, 1 - x)
-        g["u1"] = push(seg(j, s), seg(j, s), y_up)
-        g["d1"] = push(seg(j, s), seg(j, s), y_dn)
         pass_on(j, s)
 
     def stage_fwd(j):
@@ -332,7 +349,7 @@
         pass_on(j, own(2, 1 - x))
 
     def stage_out(j):
-        ubuf = bufs[j]["ubuf"]
+        ubuf = ubufs[j]
         at, h = PARTS[j]
         for cp in gats[j]["share"]:
             cp.wait_recv()
@@ -343,7 +360,7 @@
             rows = slice(first, first + h - skip)
             outv[rows, :] = coeffs[rows, :] + upd[s * h + skip:(s + 1) * h]
 
-    stages = [stage_x, stage_swap, stage_u, stage_y, stage_fwd, stage_last, stage_out]
+    stages = [stage_u, stage_y, stage_fwd, stage_last, stage_out]
     for t in range(n_parts + len(stages) - 1):
         for k, stage in enumerate(stages):
             if 0 <= t - k < n_parts:
@@ -361,20 +378,21 @@
     vm = pltpu.VMEM
     scratch = [
         vm((2, local, feat), BF16), vm((2, block), jnp.int32), vm((2, labels, local), BF16), vm((labels, local), F32),
-        vm((2, block, block), F32), vm((2, labels, local), BF16), vm((2, local, block), BF16), vm((2, local, block), BF16),
-        vm((2, local, block), BF16), vm((2, 8, 128, LANES), BF16), vm((8, 64, LANES), BF16), vm((8, 64, LANES), BF16),
+        vm((2, block, block), F32), vm((2, labels, local), BF16), vm((2, local, block), BF16),
+        vm((2, 8, 128, LANES), BF16), vm((8, 64, LANES), BF16), vm((8, 64, LANES), BF16),
         vm((7, 64, LANES), BF16), vm((64, LANES), BF16), vm((2, 8, block, LANES), BF16),
         vm((4, block, block), BF16), vm((2, local, 1), F32),
-        pltpu.SemaphoreType.DMA((5,)),
+        pltpu.SemaphoreType.DMA((5,)), pltpu.SemaphoreType.DMA((8,)),
         pltpu.SemaphoreType.DMA((COPIES,)), pltpu.SemaphoreType.DMA((COPIES,)),
     ]
-    for _, h in PARTS:
+    w = block // 2
+    for _ in range(2):
         scratch += [
-            vm((8, h, block), F32),
-            vm((2, h, block), BF16), vm((2, h, block), BF16), vm((4, h, block), BF16), vm((2, 2, h, block), BF16),
-            vm((h, block), BF16), vm((h, block), BF16), vm((h, block), F32), vm((h, block), F32),
-            vm((2, 8, h, block), BF16),
+            vm((2, local, w), BF16), vm((2, local, w), BF16), vm((8, SLAB, w), F32),
+            vm((2, SLAB, w), BF16), vm((2, SLAB, w), BF16), vm((4, SLAB, w), BF16), vm((2, 2, SLAB, w), BF16),
+            vm((SLAB, w), BF16), vm((SLAB, w), BF16), vm((SLAB, w), F32), vm((SLAB, w), F32),
         ]
+    scratch += [vm((2, 8, h, block), BF16) for _, h in PARTS]
     in_vmem = pl.BlockSpec(memory_space=pltpu.VMEM)
     in_any = pl.BlockSpec(memory_space=pltpu.HBM)
     out = pl.pallas_call(

time: 73.2 us -> 71.8 us (0.981)
  Pallas kernels: 71.5 us -> 70.2 us
    pallas_call x1, Pallas kernels: 71.5 us -> 70.2 us  [per_device(): pl.pallas_call(body, out_shape=jax.ShapeDtypeStruct((labels, local), F32)...]
where the time goes in v6:
time: 71.8 us; the launch traced here: 71.7 us
  Pallas kernels  70.2 us (98%)
  local copies, waits for them, and re-layouts  1.54 us (2%)
    pallas_call x1, Pallas kernels, per_device(): pl.pallas_call(body, out_shape=jax.ShapeDtypeStruct((labels, local), F32)...  70.2 us
    unnamed x1, local copies, waits for them, and re-layouts  1.54 us

profile of v6, /device:TPU:1, one launch (start us, length us, event | category | flops | bytes accessed | tf_op | source)
XLA Modules:
  0.0 71.7 jit_solution(9598916915950328136)
XLA Ops:
  0.0 70.2 %descent.1 = f32[1344,512]{1,0:T(8,128)S(1)} custom-call(bf16[512,1024]{1,0:T(8,128)(2,1)} %points_hbm.1, s32[2,512]{1,0:T(2,128)} %ids_hbm.1, bf16[1344,512]{1,0:T(8,128)(2,1)} %bitcast.5, f32[1344,512]{1,0:T(8,128)} %bitcast.4, f32[2,512,512]{2,1,0:T(8,128)} %inverses_hbm.1), custom_call_target="tpu_custom_call" | custom-call | tf_op jit(solution)/shard_map/descent/pallas_call | solution.py:398
  70.2 1.5 %copy.7 = f32[512,1344]{0,1:T(8,128)} copy(f32[512,1344]{0,1:T(8,128)S(1)} %bitcast.3) | data formatting | bytes 5505024

commit v7 on v6

--- a/solution.py
+++ b/solution.py
@@ -90,8 +90,8 @@
         pltpu.make_async_copy(points_hbm, points.at[core], load_sem.at[3]),
         pltpu.make_async_copy(ids_hbm, ids, load_sem.at[4]),
     ]
-    for ld in loads[::-1]:
-        ld.start()
+    loads[4].start()
+    loads[3].start()
 
     barrier = pltpu.get_barrier_semaphore()
     greet = [partner, z_up, z_dn] + [chip_peer(d) for d in range(1, 8)]
@@ -114,6 +114,8 @@
 
     loads[4].wait()
     loads[3].wait()
+    for ld in (loads[1], loads[0], loads[2]):
+        ld.start()
     z_lanes = pl.ds(pl.multiple_of((z // 2) * 128, 128), 128)
     z_half = pl.ds(pl.multiple_of((z % 2) * 64, 64), 64)
     for b in range(2):
@@ -220,6 +222,11 @@
 
     pair = z // 2 + 4
     lean = 2 * (z % 2) - 1
+    def arrival_rows(b):
+        order = (pair, pair + lean, pair - lean, pair + 2)
+        return jnp.concatenate(
+            [inverses[b, pl.ds(pl.multiple_of((g % 4) * 128, 128), 128), :] for g in order], axis=0)
+
     hops = {}
     for s in range(1, 5):
         for h in range(4):
@@ -238,6 +245,10 @@
                 point_norms[o] = col_norms(points[o])
         elif s == 2:
             fill_tile(0, 0, pair)
+            loads[2].wait()
+            hi, lo = split(arrival_rows(core))
+            weights[0] = hi
+            weights[1] = lo
             for b in range(2):
                 sel[b] = one_hot(sub_row, ids[b:b + 1, :]).astype(BF16)
         elif s == 3:
@@ -247,8 +258,8 @@
             stage_far(0)
             stage_near(0)
         else:
+            stage_dep(0)
             fill_tile(1, 0, pair - lean)
-            stage_dep(0)
     for sign, hs in ((1, (0, 1)), (-1, (2, 3))):
         for h in hs:
             hops[sign, 4, h].wait_recv()
@@ -265,22 +276,12 @@
     ids0 = jnp.sum(jnp.where(eye, ids[0:1, :].astype(F32), 0.0), axis=1, keepdims=True)
     same = one_hot(ids0, ids[1:2, :].astype(F32))
     cross = (gauss(q0, col_norms(q0), q1, row_norms(q1)).astype(F32) + RIDGE * same).astype(BF16)
-    loads[2].wait()
-
-    def arrival_rows(b):
-        order = (pair, pair + lean, pair - lean, pair + 2)
-        return jnp.concatenate(
-            [inverses[b, pl.ds(pl.multiple_of((g % 4) * 128, 128), 128), :] for g in order], axis=0)
-
     hi, lo = split(arrival_rows(0))
     b_hi, b_lo = split(mm(hi, cross) + mm(lo, cross))
     hi, lo = split(inverses[1])
     c_hi, c_lo = split(jnp.where(core == 1, mm(b_hi, hi) + mm(b_hi, lo) + mm(b_lo, hi), 0.0))
     weights[2] = c_hi
     weights[3] = c_lo
-    hi, lo = split(arrival_rows(core))
-    weights[0] = hi
-    weights[1] = lo
 
     def own(step, xx):
         return ((y + step) % 4) * 2 + xx
@@ -292,7 +293,8 @@
 
     def times(n, w_hi, w_lo):
         hi, lo = split(n)
-        return mm(hi, w_hi) + mm(lo, w_hi) + mm(hi, w_lo)
+        both = mm(jnp.concatenate([hi, lo], axis=0), w_hi)
+        return both[:n.shape[0]] + both[n.shape[0]:] + mm(hi, w_lo)
 
     def pass_on(j, s):
         gats[j]["share"].append(push(seg(j, s), seg(j, s), partner))

time: 71.8 us -> 71.1 us (level)
  Pallas kernels: 70.2 us -> 69.4 us
    pallas_call x1, Pallas kernels: 70.2 us -> 69.4 us  [per_device(): pl.pallas_call(body, out_shape=jax.ShapeDtypeStruct((labels, local), F32)...]
where the time goes in v7:
time: 71.1 us; the launch traced here: 71 us
  Pallas kernels  69.4 us (98%)
  local copies, waits for them, and re-layouts  1.54 us (2%)
    pallas_call x1, Pallas kernels, per_device(): pl.pallas_call(body, out_shape=jax.ShapeDtypeStruct((labels, local), F32)...  69.4 us
    unnamed x1, local copies, waits for them, and re-layouts  1.54 us

profile of v7, /device:TPU:1, one launch (start us, length us, event | category | flops | bytes accessed | tf_op | source)
XLA Modules:
  0.0 71.0 jit_solution(5723321801626428835)
XLA Ops:
  0.0 69.4 %descent.1 = f32[1344,512]{1,0:T(8,128)S(1)} custom-call(bf16[512,1024]{1,0:T(8,128)(2,1)} %points_hbm.1, s32[2,512]{1,0:T(2,128)} %ids_hbm.1, bf16[1344,512]{1,0:T(8,128)(2,1)} %bitcast.5, f32[1344,512]{1,0:T(8,128)} %bitcast.4, f32[2,512,512]{2,1,0:T(8,128)} %inverses_hbm.1), custom_call_target="tpu_custom_call" | custom-call | tf_op jit(solution)/shard_map/descent/pallas_call | solution.py:400
  69.4 1.5 %copy.7 = f32[512,1344]{0,1:T(8,128)} copy(f32[512,1344]{0,1:T(8,128)S(1)} %bitcast.3) | data formatting | bytes 5505024

commit v8 on v7

--- a/solution.py
+++ b/solution.py
@@ -11,9 +11,9 @@
 MESH = pl.DeviceIdType.MESH
 F32, BF16 = jnp.float32, jnp.bfloat16
 LANES = 128
-PARTS = ((0, 64), (64, 64), (128, 48))
+PARTS = ((0, 48), (48, 48), (96, 48), (144, 32))
 SLAB = 176
-COPIES = 176
+COPIES = 200
 NT = (((1,), (1,)), ((), ()))
 TN = (((0,), (0,)), ((), ()))
 

time: 71.1 us -> 71.8 us (level)
  Pallas kernels: 69.4 us -> 70.2 us
    pallas_call x1, Pallas kernels: 69.4 us -> 70.2 us  [per_device(): pl.pallas_call(body, out_shape=jax.ShapeDtypeStruct((labels, local), F32)...]
where the time goes in v8:
time: 71.8 us; the launch traced here: 71.7 us
  Pallas kernels  70.2 us (98%)
  local copies, waits for them, and re-layouts  1.54 us (2%)
    pallas_call x1, Pallas kernels, per_device(): pl.pallas_call(body, out_shape=jax.ShapeDtypeStruct((labels, local), F32)...  70.2 us
    unnamed x1, local copies, waits for them, and re-layouts  1.54 us

profile of v8, /device:TPU:1, one launch (start us, length us, event | category | flops | bytes accessed | tf_op | source)
XLA Modules:
  0.0 71.7 jit_solution(9792832745848756495)
XLA Ops:
  0.0 70.2 %descent.1 = f32[1344,512]{1,0:T(8,128)S(1)} custom-call(bf16[512,1024]{1,0:T(8,128)(2,1)} %points_hbm.1, s32[2,512]{1,0:T(2,128)} %ids_hbm.1, bf16[1344,512]{1,0:T(8,128)(2,1)} %bitcast.5, f32[1344,512]{1,0:T(8,128)} %bitcast.4, f32[2,512,512]{2,1,0:T(8,128)} %inverses_hbm.1), custom_call_target="tpu_custom_call" | custom-call | tf_op jit(solution)/shard_map/descent/pallas_call | solution.py:400
  70.2 1.5 %copy.7 = f32[512,1344]{0,1:T(8,128)} copy(f32[512,1344]{0,1:T(8,128)S(1)} %bitcast.3) | data formatting | bytes 5505024
